TPU v7x, 32 devices: a whole 2x2x4 slice. The times are simulated.
32 devices in a mesh: dp: 8 (over z, x), mp: 4 (over y, core).
Axes of the slice: x: 2, y: 2, z: 4, core: 2. Of those that a mesh axis runs over, the one named last changes fastest.
Arguments:
- patches: bfloat16 [8, 2048, 768], P('dp'), may hold values from -6 to 6
- cotangent: bfloat16 [8, 2048, 768], P('dp'), may hold values from -6 to 6
- keep_mask: int32 [8, 2048], P('dp'), may hold values from 0 to 1, as said below
- segment_ids: int32 [8, 2048], P('dp'), may hold values from 0 to 7, never falling along the last dimension, each value on 1 to 512 neighbouring positions
- step_count: int32 [1], replicated, may hold values from 2 to 8
- qkv_weight: float32 [3, 768, 768], P(None, None, 'mp'), may hold values from -0.21875 to 0.21875
- qkv_first: float32 [3, 768, 768], P(None, 'dp', 'mp'), may hold values from -0.00061035156 to 0.00061035156
- qkv_second: float32 [3, 768, 768], P(None, 'dp', 'mp'), may hold values from 7.4315953e-09 to 2.9669868e-08
- out_weight: float32 [768, 768], P('mp'), may hold values from -1.75 to 1.75
- out_first: float32 [768, 768], P('mp', 'dp'), may hold values from -0.00061035156 to 0.00061035156
- out_second: float32 [768, 768], P('mp', 'dp'), may hold values from 7.4315953e-09 to 2.9669868e-08
- up_weight: float32 [768, 3072], P(None, 'mp'), may hold values from -0.21875 to 0.21875
- up_first: float32 [768, 3072], P('dp', 'mp'), may hold values from -0.00061035156 to 0.00061035156
- up_second: float32 [768, 3072], P('dp', 'mp'), may hold values from 7.4315953e-09 to 2.9669868e-08
- down_weight: float32 [3072, 768], P('mp'), may hold values from -0.109375 to 0.109375
- down_first: float32 [3072, 768], P('mp', 'dp'), may hold values from -0.00061035156 to 0.00061035156
- down_second: float32 [3072, 768], P('mp', 'dp'), may hold values from 7.4315953e-09 to 2.9669868e-08
- head_params: float32 [5, 12, 64], P(None, 'mp'), may hold values from -2 to 2, as said below
- head_first: float32 [5, 12, 64], P(None, 'mp'), may hold values from -0.00061035156 to 0.00061035156
- head_second: float32 [5, 12, 64], P(None, 'mp'), may hold values from 7.4315953e-09 to 2.9669868e-08
- up_bias: float32 [3072], P('mp'), may hold values from -2 to 2
- upb_first: float32 [3072], P('mp'), may hold values from -0.00061035156 to 0.00061035156
- upb_second: float32 [3072], P('mp'), may hold values from 7.4315953e-09 to 2.9669868e-08
- vec_params: float32 [6, 768], replicated, may hold values from -2 to 2, as said below
- vec_first: float32 [6, 768], replicated, may hold values from -0.00061035156 to 0.00061035156
- vec_second: float32 [6, 768], replicated, may hold values from 7.4315953e-09 to 2.9669868e-08
Outputs:
- block_out: bfloat16 [8, 2048, 768], P('dp')
- grad_input: bfloat16 [8, 2048, 768], P('dp')
- new_qkv: float32 [3, 768, 768], P(None, 'dp', 'mp')
- new_qkv_first: float32 [3, 768, 768], P(None, 'dp', 'mp')
- new_qkv_second: float32 [3, 768, 768], P(None, 'dp', 'mp')
- new_out: float32 [768, 768], P('mp', 'dp')
- new_out_first: float32 [768, 768], P('mp', 'dp')
- new_out_second: float32 [768, 768], P('mp', 'dp')
- new_up: float32 [768, 3072], P('dp', 'mp')
- new_up_first: float32 [768, 3072], P('dp', 'mp')
- new_up_second: float32 [768, 3072], P('dp', 'mp')
- new_down: float32 [3072, 768], P('mp', 'dp')
- new_down_first: float32 [3072, 768], P('mp', 'dp')
- new_down_second: float32 [3072, 768], P('mp', 'dp')
- new_head: float32 [5, 12, 64], P(None, 'mp')
- new_head_first: float32 [5, 12, 64], P(None, 'mp')
- new_head_second: float32 [5, 12, 64], P(None, 'mp')
- new_upb: float32 [3072], P('mp')
- new_upb_first: float32 [3072], P('mp')
- new_upb_second: float32 [3072], P('mp')
- new_vec: float32 [6, 768], replicated
- new_vec_first: float32 [6, 768], replicated
- new_vec_second: float32 [6, 768], replicated
- grad_norm: float32 [1], replicated
- rms_stats: float32 [2], replicated
Inputs may be any that keep to these rules, and one draw needn't show every extreme that they name: `keep_mask`: per sequence each patch is kept with a chance from one half to all; the chance rises with the sequence index. `segment_ids`: within a row ids never fall; each image covers 1 to 512 consecutive slots, one exactly that many. `head_params`: rows 0 to 2 are biases, rows 3 and 4 gains. `vec_params`: rows 0 and 2 are gains, the others biases.
All inputs are finite; a program needn't handle non-finite values.
Results may differ from a plain program's by a relative error of at most 0.012.
Values sent between devices are 32-bit elements; how exact they have to be, the bound alone decides.
No kernel may reach another device: no remote copies, remote signals or barrier semaphores. Data moves between devices by JAX's collectives and lax.ppermute only.
A program may use at most 256 MiB of HBM per device.

v0:
```python
import jax
import jax.numpy as jnp
from jax import lax
from jax.sharding import PartitionSpec as P

NORM_EPS = 1e-06
CLIP_LIMIT = 1.0
LEARN_RATE = 0.1
BETA_ONE = 0.9
BETA_TWO = 0.95
ADAM_EPS = 1e-08
WEIGHT_DECAY = 0.1


def standardize(values):
    center = values - jnp.mean(values, axis=-1, keepdims=True)
    spread = jnp.mean(center * center, axis=-1, keepdims=True)
    factor = lax.rsqrt(spread + NORM_EPS)
    return (center * factor, factor)


def norm_back(grad_hat, normed, factor):
    return factor * (
        grad_hat
        - jnp.mean(grad_hat, axis=-1, keepdims=True)
        - normed * jnp.mean(grad_hat * normed, axis=-1, keepdims=True)
    )


def adam_step(weight, grad, first, second, factor, corr_one, corr_two, decay):
    grad = factor * grad
    first = BETA_ONE * first + (1.0 - BETA_ONE) * grad
    second = BETA_TWO * second + (1.0 - BETA_TWO) * grad * grad
    update = first / corr_one / (jnp.sqrt(second / corr_two) + ADAM_EPS)
    return (weight - LEARN_RATE * (update + decay * weight), first, second)


def local(
    patches,
    cotangent,
    keep_mask,
    segment_ids,
    step_count,
    qkv_weight,
    qkv_first,
    qkv_second,
    out_weight,
    out_first,
    out_second,
    up_weight,
    up_first,
    up_second,
    down_weight,
    down_first,
    down_second,
    head_params,
    head_first,
    head_second,
    up_bias,
    upb_first,
    upb_second,
    vec_params,
    vec_first,
    vec_second,
):
    seq_len = patches.shape[1]
    width = patches.shape[2]
    heads_here = head_params.shape[1]
    head_dim = head_params.shape[2]
    local_width = heads_here * head_dim
    head_scale = head_dim ** (-0.5)
    inputs = patches[0].astype(jnp.float32)
    keep_row = keep_mask[0]
    seg_row = segment_ids[0]
    keep_f = keep_row.astype(jnp.float32)
    places = jnp.arange(seq_len)
    xh_first, rs_first = standardize(inputs)
    a_first = (xh_first * vec_params[0] + vec_params[1]).astype(jnp.bfloat16)
    qkv_low = qkv_weight.astype(jnp.bfloat16)
    raw = jnp.einsum("sd,kde->kse", a_first, qkv_low, preferred_element_type=jnp.float32)
    raw = raw + head_params[0:3].reshape(3, 1, local_width)
    query = raw[0].reshape(seq_len, heads_here, head_dim)
    key_raw = raw[1].reshape(seq_len, heads_here, head_dim)
    value = raw[2].reshape(seq_len, heads_here, head_dim)
    q_hat, q_factor = standardize(query)
    k_hat, k_factor = standardize(key_raw)
    q_in = (q_hat * head_params[3] * head_scale).astype(jnp.bfloat16)
    k_in = (k_hat * head_params[4]).astype(jnp.bfloat16)
    v_in = value.astype(jnp.bfloat16)
    block = min(512, seq_len)
    blocks = seq_len // block

    def block_scores(start):
        q_block = q_in[start : start + block]
        scores = jnp.einsum("qhd,khd->hqk", q_block, k_in, preferred_element_type=jnp.float32)
        allowed = (seg_row[start : start + block, None] == seg_row[None, :]) & (
            (keep_row[None, :] == 1) | (places[start : start + block, None] == places[None, :])
        )
        return (jnp.where(allowed[None], scores, -1e30), q_block)

    outs_list = []
    lse_list = []
    for index in range(blocks):
        scores, q_block = block_scores(index * block)
        top = jnp.max(scores, axis=-1, keepdims=True)
        expo = jnp.exp(scores - top)
        total = jnp.sum(expo, axis=-1, keepdims=True)
        probs = (expo / total).astype(jnp.bfloat16)
        lse_list.append(top + jnp.log(total))
        outs_list.append(
            jnp.einsum("hqk,khd->qhd", probs, v_in, preferred_element_type=jnp.float32)
        )
    mixed = jnp.concatenate(outs_list, axis=0).reshape(seq_len, local_width).astype(jnp.bfloat16)
    out_low = out_weight.astype(jnp.bfloat16)
    attn = (
        lax.psum(jnp.dot(mixed, out_low, preferred_element_type=jnp.float32), "mp") + vec_params[4]
    )
    hidden = inputs + attn
    xh_second, rs_second = standardize(hidden)
    a_second = (xh_second * vec_params[2] + vec_params[3]).astype(jnp.bfloat16)
    up_low = up_weight.astype(jnp.bfloat16)
    upper = jnp.dot(a_second, up_low, preferred_element_type=jnp.float32) + up_bias
    gelu_value, gelu_back = jax.vjp(lambda val: jax.nn.gelu(val, approximate=False), upper)
    gated = gelu_value.astype(jnp.bfloat16)
    down_low = down_weight.astype(jnp.bfloat16)
    mlp = (
        lax.psum(jnp.dot(gated, down_low, preferred_element_type=jnp.float32), "mp") + vec_params[5]
    )
    result = hidden + mlp
    count_here = jnp.sum(keep_f)
    attn_sq = jnp.sum(keep_f[:, None] * attn * attn)
    mlp_sq = jnp.sum(keep_f[:, None] * mlp * mlp)
    count, attn_total, mlp_total = lax.psum((count_here, attn_sq, mlp_sq), "dp")
    grad_out = cotangent[0].astype(jnp.float32) * keep_f[:, None]
    grad_mlp = grad_out.astype(jnp.bfloat16)
    grad_bdown = jnp.sum(grad_mlp.astype(jnp.float32), axis=0)
    grad_down = jnp.einsum("sf,sd->fd", gated, grad_mlp, preferred_element_type=jnp.float32)
    grad_gated = jnp.einsum("sd,fd->sf", grad_mlp, down_low, preferred_element_type=jnp.float32)
    grad_upper = gelu_back(grad_gated)[0].astype(jnp.bfloat16)
    grad_bup = jnp.sum(grad_upper.astype(jnp.float32), axis=0)
    grad_up = jnp.einsum("sd,sf->df", a_second, grad_upper, preferred_element_type=jnp.float32)
    grad_xn2 = lax.psum(
        jnp.einsum("sf,df->sd", grad_upper, up_low, preferred_element_type=jnp.float32), "mp"
    )
    grad_gain2 = jnp.sum(grad_xn2 * xh_second, axis=0)
    grad_bias2 = jnp.sum(grad_xn2, axis=0)
    grad_hidden = grad_out + norm_back(grad_xn2 * vec_params[2], xh_second, rs_second)
    grad_attn = grad_hidden.astype(jnp.bfloat16)
    grad_bout = jnp.sum(grad_attn.astype(jnp.float32), axis=0)
    grad_outw = jnp.einsum("se,sd->ed", mixed, grad_attn, preferred_element_type=jnp.float32)
    grad_mixed = jnp.einsum("sd,ed->se", grad_attn, out_low, preferred_element_type=jnp.float32)
    grad_mixed = grad_mixed.astype(jnp.bfloat16).reshape(seq_len, heads_here, head_dim)
    grad_kin = jnp.zeros((seq_len, heads_here, head_dim), jnp.float32)
    grad_vin = jnp.zeros((seq_len, heads_here, head_dim), jnp.float32)
    grad_qlist = []
    for index in range(blocks):
        start = index * block
        scores, q_block = block_scores(start)
        probs_full = jnp.exp(scores - lse_list[index])
        probs = probs_full.astype(jnp.bfloat16)
        grad_block = grad_mixed[start : start + block]
        grad_vin = grad_vin + jnp.einsum(
            "hqk,qhd->khd", probs, grad_block, preferred_element_type=jnp.float32
        )
        grad_probs = jnp.einsum(
            "qhd,khd->hqk", grad_block, v_in, preferred_element_type=jnp.float32
        )
        delta = jnp.sum(probs_full * grad_probs, axis=-1, keepdims=True)
        grad_scores = (probs_full * (grad_probs - delta)).astype(jnp.bfloat16)
        grad_qlist.append(
            jnp.einsum("hqk,khd->qhd", grad_scores, k_in, preferred_element_type=jnp.float32)
        )
        grad_kin = grad_kin + jnp.einsum(
            "hqk,qhd->khd", grad_scores, q_block, preferred_element_type=jnp.float32
        )
    grad_qin = jnp.concatenate(grad_qlist, axis=0) * head_scale
    grad_qgain = jnp.sum(grad_qin * q_hat, axis=0)
    grad_query = norm_back(grad_qin * head_params[3], q_hat, q_factor)
    grad_kgain = jnp.sum(grad_kin * k_hat, axis=0)
    grad_key = norm_back(grad_kin * head_params[4], k_hat, k_factor)
    grad_raw = jnp.stack(
        [
            grad_query.reshape(seq_len, local_width),
            grad_key.reshape(seq_len, local_width),
            grad_vin.reshape(seq_len, local_width),
        ]
    ).astype(jnp.bfloat16)
    grad_bqkv = jnp.sum(grad_raw.astype(jnp.float32), axis=1)
    grad_qkv = jnp.einsum("sd,kse->kde", a_first, grad_raw, preferred_element_type=jnp.float32)
    grad_xn1 = lax.psum(
        jnp.einsum("kse,kde->sd", grad_raw, qkv_low, preferred_element_type=jnp.float32), "mp"
    )
    grad_gain1 = jnp.sum(grad_xn1 * xh_first, axis=0)
    grad_bias1 = jnp.sum(grad_xn1, axis=0)
    grad_inputs = grad_hidden + norm_back(grad_xn1 * vec_params[0], xh_first, rs_first)
    vec_grad = jnp.stack([grad_gain1, grad_bias1, grad_gain2, grad_bias2, grad_bout, grad_bdown])
    head_grad = jnp.concatenate(
        [grad_bqkv.reshape(3, heads_here, head_dim), jnp.stack([grad_qgain, grad_kgain])], axis=0
    )
    vec_grad, head_grad, bup_grad = lax.psum((vec_grad, head_grad, grad_bup), "dp")
    dp_rank = lax.axis_index("dp")
    rows = width // lax.axis_size("dp")
    start_row = dp_rank * rows
    summed = lax.psum((grad_qkv, grad_outw, grad_up, grad_down), "dp")
    shares = (
        lax.dynamic_slice_in_dim(summed[0], start_row, rows, 1),
        lax.dynamic_slice_in_dim(summed[1], start_row, rows, 1),
        lax.dynamic_slice_in_dim(summed[2], start_row, rows, 0),
        lax.dynamic_slice_in_dim(summed[3], start_row, rows, 1),
    )
    old_shares = (
        lax.dynamic_slice_in_dim(qkv_weight, start_row, rows, 1),
        lax.dynamic_slice_in_dim(out_weight, start_row, rows, 1),
        lax.dynamic_slice_in_dim(up_weight, start_row, rows, 0),
        lax.dynamic_slice_in_dim(down_weight, start_row, rows, 1),
    )
    first_dp = dp_rank == 0
    first_mp = lax.axis_index("mp") == 0
    big_sq = sum((jnp.sum(share * share) for share in shares))
    split_sq = jnp.sum(head_grad * head_grad) + jnp.sum(bup_grad * bup_grad)
    whole_sq = jnp.sum(vec_grad * vec_grad)
    raw_sq = (
        big_sq + jnp.where(first_dp, split_sq, 0.0) + jnp.where(first_dp & first_mp, whole_sq, 0.0)
    )
    sq_total = lax.psum(raw_sq, ("dp", "mp"))
    scale = seq_len * lax.axis_size("dp") / count
    grad_norm = scale * jnp.sqrt(sq_total)
    factor = jnp.minimum(1.0, CLIP_LIMIT / (grad_norm + 1e-06)) * scale
    steps_f = step_count[0].astype(jnp.float32)
    corr_one = 1.0 - BETA_ONE**steps_f
    corr_two = 1.0 - BETA_TWO**steps_f
    new_qkv = adam_step(
        old_shares[0], shares[0], qkv_first, qkv_second, factor, corr_one, corr_two, WEIGHT_DECAY
    )
    new_out = adam_step(
        old_shares[1], shares[1], out_first, out_second, factor, corr_one, corr_two, WEIGHT_DECAY
    )
    new_up = adam_step(
        old_shares[2], shares[2], up_first, up_second, factor, corr_one, corr_two, WEIGHT_DECAY
    )
    new_down = adam_step(
        old_shares[3], shares[3], down_first, down_second, factor, corr_one, corr_two, WEIGHT_DECAY
    )
    new_head = adam_step(
        head_params, head_grad, head_first, head_second, factor, corr_one, corr_two, 0.0
    )
    new_upb = adam_step(up_bias, bup_grad, upb_first, upb_second, factor, corr_one, corr_two, 0.0)
    new_vec = adam_step(
        vec_params, vec_grad, vec_first, vec_second, factor, corr_one, corr_two, 0.0
    )
    rms = jnp.sqrt(jnp.stack([attn_total, mlp_total]) / (count * width))
    return (
        result.astype(jnp.bfloat16)[None],
        (grad_inputs * scale).astype(jnp.bfloat16)[None],
        new_qkv[0],
        new_qkv[1],
        new_qkv[2],
        new_out[0],
        new_out[1],
        new_out[2],
        new_up[0],
        new_up[1],
        new_up[2],
        new_down[0],
        new_down[1],
        new_down[2],
        new_head[0],
        new_head[1],
        new_head[2],
        new_upb[0],
        new_upb[1],
        new_upb[2],
        new_vec[0],
        new_vec[1],
        new_vec[2],
        grad_norm.reshape(1),
        rms,
    )


def solution(mesh):
    placed = (
        P("dp", None, None),
        P("dp", None, None),
        P("dp", None),
        P("dp", None),
        P(),
        P(None, None, "mp"),
        P(None, "dp", "mp"),
        P(None, "dp", "mp"),
        P("mp", None),
        P("mp", "dp"),
        P("mp", "dp"),
        P(None, "mp"),
        P("dp", "mp"),
        P("dp", "mp"),
        P("mp", None),
        P("mp", "dp"),
        P("mp", "dp"),
        P(None, "mp", None),
        P(None, "mp", None),
        P(None, "mp", None),
        P("mp"),
        P("mp"),
        P("mp"),
        P(),
        P(),
        P(),
    )
    return jax.shard_map(
        local,
        mesh=mesh,
        in_specs=placed,
        out_specs=(
            P("dp", None, None),
            P("dp", None, None),
            P(None, "dp", "mp"),
            P(None, "dp", "mp"),
            P(None, "dp", "mp"),
            P("mp", "dp"),
            P("mp", "dp"),
            P("mp", "dp"),
            P("dp", "mp"),
            P("dp", "mp"),
            P("dp", "mp"),
            P("mp", "dp"),
            P("mp", "dp"),
            P("mp", "dp"),
            P(None, "mp", None),
            P(None, "mp", None),
            P(None, "mp", None),
            P("mp"),
            P("mp"),
            P("mp"),
            P(),
            P(),
            P(),
            P(),
            P(),
        ),
        check_vma=False,
    )
```

profile of v0, /device:TPU:0, one launch (start us, length us, event | category | flops | bytes accessed | tf_op | source)
XLA Modules:
  0.0 1092.1 jit_solution(17115793789987397871)
XLA Ops:
  52.6 7.8 fusion.3
  67.2 7.8 fusion.2
  88.1 7.8 fusion.1
  95.8 6.8 fusion.95
  109.5 7.8 fusion
  128.5 122.3 %all-reduce.8.cloned.1.call-done = f32[2048,768]{1,0:T(8,128)} async-done(((f32[2048,768]{1,0:T(8,128)}), f32[2048,768]{1,0:T(8,128)}) %all-reduce.8.cloned.1.call-update) | async-done | bytes 6291472 | tf_op jit(solution)/shard_map/psum | solution.py:116
  258.4 17.7 %multiply_convert_fusion.4 = (bf16[2048,768]{1,0:T(8,128)(2,1)}, f32[2048,768]{1,0:T(8,128)}, f32[2048,768]{1,0:T(8,128)}) fusion(f32[768]{0:T(1024)S(1)} %copy-done.103, bf16[2048,768]{1,0:T(8,128)(2,1)S(1)} %add_convert_fusion.2, f32[768,768]{1,0:T(8,128)S(1)} %copy-done.84), kind=kOutput, calls=%fused_computation.76 | convolution fusion | flops 2520317952 | bytes 21236736 | tf_op jit(solution)/shard_map/dot_general | solution.py:122
  276.1 8.2 convert_reduce_fusion.3
  293.6 8.1 fusion.101
  301.7 108.6 %all-reduce.10.cloned.1.call-done = f32[2048,768]{1,0:T(8,128)} async-done(((f32[2048,768]{1,0:T(8,128)}), f32[2048,768]{1,0:T(8,128)}) %all-reduce.10.cloned.1.call-update) | async-done | bytes 6291472 | tf_op jit(solution)/shard_map/psum | solution.py:142
  433.5 10.1 multiply_convert_fusion.3
  456.3 9.4 multiply_reduce_fusion.2
  471.5 7.4 multiply_reduce_fusion.1
  478.9 10.3 fusion.76
  489.2 8.9 multiply_reduce_fusion
  504.0 9.6 multiply_convert_fusion
  519.3 10.3 multiply_convert_fusion.2
  557.9 7.1 fusion.168
  595.3 183.7 %all-reduce.14.cloned.1.call-done = (f32[2048,768]{1,0:T(8,128)}, f32[2048,768]{1,0:T(8,128)}) async-done(((f32[2048,768]{1,0:T(8,128)}, f32[2048,768]{1,0:T(8,128)}), (f32[2048,768]{1,0:T(8,128)}, f32[2048,768]{1,0:T(8,128)})) %all-reduce.14.cloned.1.call-update) | async-done | bytes 12582928 | tf_op jit(solution)/shard_map/psum | solution.py:127
  778.9 16.2 %fusion.24 = (f32[768]{0:T(1024)S(1)}, f32[2048]{0:T(1024)S(1)}, f32[2048]{0:T(1024)S(1)}, f32[768]{0:T(1024)S(1)}, bf16[1,2048,768]{2,1,0:T(8,128)(2,1)}, /*index=5*/f32[]{:T(128)}, f32[768]{0:T(1024)S(1)}, f32[]{:T(128)}) fusion(f32[2048,768]{1,0:T(8,128)} %get-tuple-element.83, bf16[1,2048,768]{2,1,0:T(8,128)(2,1)S(1)} %copy-done.6, ...), kind=kLoop, calls=%fused_computation.53 | loop fusion | flops 39315200 | bytes 34662408 | tf_op jit(solution)/shard_map/reduce_sum | solution.py:193
  795.2 41.8 %all-reduce = (f32[]{:T(128)}, f32[5,3,64]{2,1,0:T(4,128)S(1)}, f32[768]{0:T(1024)S(1)}, f32[6,768]{1,0:T(8,128)S(1)}, f32[1]{0:T(128)}, /*index=5*/f32[1]{0:T(128)}) all-reduce(f32[]{:T(128)} %convert_reduce_fusion.5, f32[5,3,64]{2,1,0:T(4,128)S(1)} %pad_maximum_fusion.3, ...), channel_id=1, replica_groups=mesh['dp'=8,'mp'=4] {'dp'}, use_global_device_ids=true, to_apply=%region_33.34 | all-reduce | flops 6339 | bytes 50712 | tf_op jit(solution)/shard_map/psum | solution.py:133
  842.2 7.1 fusion.71
  849.4 171.1 %all-reduce.12.cloned.1.call-done = (f32[3,768,192]{1,2,0:T(8,128)}, f32[192,768]{1,0:T(8,128)}, f32[768,768]{1,0:T(8,128)}, f32[768,768]{0,1:T(8,128)}) async-done(((f32[3,768,192]{1,2,0:T(8,128)}, f32[192,768]{1,0:T(8,128)}, f32[768,768]{1,0:T(8,128)}, f32[768,768]{0,1:T(8,128)}), (f32[3,768,192]{1,2,0:T(8,128)}, f32[192,768]{1,0:T(8,128)}, f32[768,768]{1,0:T(8,128)}, ...) | async-done | bytes 7077904 | tf_op jit(solution)/shard_map/psum | solution.py:204
  1031.7 39.1 %psum.117 = f32[]{:T(128)} all-reduce(f32[]{:T(128)S(6)} %add.375), channel_id=1, replica_groups=mesh['dp'=8,'mp'=4] {'dp','mp'}, use_global_device_ids=true, to_apply=%region_58.59 | all-reduce | flops 1 | bytes 8 | tf_op jit(solution)/shard_map/psum | solution.py:225
  (394 shorter events, 232.9 us)
Async XLA Ops:
  7.2 243.6 %all-reduce.8.cloned.1.call-start = ((), (), s32[]{:S(2)}) async-start(), calls=%async_computation | async-start | bytes 12582912 | tf_op jit(solution)/shard_map/psum | solution.py:116
  15.7 235.1 %copy-start.85 = (f32[768]{0:T(1024)}, f32[768]{0:T(1024)S(1)}, u32[]{:S(2)}) copy-start(f32[768]{0:T(1024)S(1)} %get-tuple-element.66) | copy-start | bytes 9220
  31.1 71.6 %copy-start.29 = (bf16[2048,3,64]{0,2,1:T(8,128)(2,1)}, bf16[2048,3,64]{0,2,1:T(8,128)(2,1)S(1)}, u32[]{:S(2)}) copy-start(bf16[2048,3,64]{0,2,1:T(8,128)(2,1)S(1)} %multiply_convert_fusion.7) | copy-start | bytes 2359300
  39.3 77.9 %copy-start.15 = (pred[512,2048]{1,0:T(8,128)(4,1)}, pred[512,2048]{1,0:T(8,128)(4,1)S(1)}, u32[]{:S(2)}) copy-start(pred[512,2048]{1,0:T(8,128)(4,1)S(1)} %get-tuple-element.123) | copy-start | bytes 3145732
  128.4 282.0 %all-reduce.10.cloned.1.call-start = ((), (), s32[]{:S(2)}) async-start(), calls=%async_computation.1 | async-start | bytes 12582912 | tf_op jit(solution)/shard_map/psum | solution.py:142
  128.4 288.8 %copy-start.74 = (f32[1,2048]{1,0:T(1,128)}, f32[1,2048]{1,0:T(1,128)S(1)}, u32[]{:S(2)}) copy-start(f32[1,2048]{1,0:T(1,128)S(1)} %convert_element_type.148) | copy-start | bytes 24580
  290.4 488.5 %all-reduce.14.cloned.1.call-start = ((), (), s32[]{:S(2)}) async-start(), calls=%async_computation.3 | async-start | bytes 25165824 | tf_op jit(solution)/shard_map/psum | solution.py:127
  293.6 139.9 %copy-start.61 = (f32[3,512]{1,0:T(4,128)}, f32[3,512]{1,0:T(4,128)S(1)}, u32[]{:S(2)}) copy-start(f32[3,512]{1,0:T(4,128)S(1)} %log_add_fusion.3) | copy-start | bytes 18436
  557.6 462.9 %all-reduce.12.cloned.1.call-start = ((), (), s32[]{:S(2)}) async-start(), calls=%async_computation.2 | async-start | bytes 14155776 | tf_op jit(solution)/shard_map/psum | solution.py:204
  842.2 229.4 %copy-start.52 = (f32[3,96,192]{1,2,0:T(8,128)S(1)}, f32[3,96,192]{1,2,0:T(8,128)}, u32[]{:S(2)}) copy-start(f32[3,96,192]{1,2,0:T(8,128)} %copy.51) | copy-start | bytes 663556
  849.3 228.8 %copy-start.66 = (f32[192,96]{1,0:T(8,128)S(1)}, f32[192,96]{1,0:T(8,128)}, u32[]{:S(2)}) copy-start(f32[192,96]{1,0:T(8,128)} %param.36) | copy-start | bytes 221188
  849.3 228.8 %copy-start.67 = (f32[192,96]{1,0:T(8,128)S(1)}, f32[192,96]{1,0:T(8,128)}, u32[]{:S(2)}) copy-start(f32[192,96]{1,0:T(8,128)} %param.35) | copy-start | bytes 221188
  849.3 230.7 %copy-start.104 = (f32[768]{0:T(1024)S(1)}, f32[768]{0:T(1024)}, u32[]{:S(2)}) copy-start(f32[768]{0:T(1024)} %param.46) | copy-start | bytes 9220
  849.3 230.7 %copy-start.105 = (f32[768]{0:T(1024)S(1)}, f32[768]{0:T(1024)}, u32[]{:S(2)}) copy-start(f32[768]{0:T(1024)} %param.48) | copy-start | bytes 9220
  849.3 230.7 %copy-start.106 = (f32[768]{0:T(1024)S(1)}, f32[768]{0:T(1024)}, u32[]{:S(2)}) copy-start(f32[768]{0:T(1024)} %param.47) | copy-start | bytes 9220
  849.3 231.3 %copy-start.80 = (f32[5,3,64]{2,1,0:T(4,128)S(1)}, f32[5,3,64]{2,1,0:T(4,128)}, u32[]{:S(2)}) copy-start(f32[5,3,64]{2,1,0:T(4,128)} %param.43) | copy-start | bytes 11524
  849.3 231.3 %copy-start.97 = (f32[5,3,64]{2,1,0:T(4,128)S(1)}, f32[5,3,64]{2,1,0:T(4,128)}, u32[]{:S(2)}) copy-start(f32[5,3,64]{2,1,0:T(4,128)} %param.45) | copy-start | bytes 11524
  849.3 231.3 %copy-start.98 = (f32[5,3,64]{2,1,0:T(4,128)S(1)}, f32[5,3,64]{2,1,0:T(4,128)}, u32[]{:S(2)}) copy-start(f32[5,3,64]{2,1,0:T(4,128)} %param.44) | copy-start | bytes 11524
  849.3 231.9 %copy-start.69 = (f32[6,768]{1,0:T(8,128)S(1)}, f32[6,768]{1,0:T(8,128)}, u32[]{:S(2)}) copy-start(f32[6,768]{1,0:T(8,128)} %param.49) | copy-start | bytes 55300
  849.3 231.9 %copy-start.92 = (f32[6,768]{1,0:T(8,128)S(1)}, f32[6,768]{1,0:T(8,128)}, u32[]{:S(2)}) copy-start(f32[6,768]{1,0:T(8,128)} %param.51) | copy-start | bytes 55300
  849.4 231.9 %copy-start.93 = (f32[6,768]{1,0:T(8,128)S(1)}, f32[6,768]{1,0:T(8,128)}, u32[]{:S(2)}) copy-start(f32[6,768]{1,0:T(8,128)} %param.50) | copy-start | bytes 55300
  849.4 232.5 %copy-start.53 = (f32[768,96]{0,1:T(8,128)S(1)}, f32[768,96]{0,1:T(8,128)}, u32[]{:S(2)}) copy-start(f32[768,96]{0,1:T(8,128)} %copy.57) | copy-start | bytes 884740
  849.4 232.5 %copy-start.62 = (f32[768,96]{0,1:T(8,128)S(1)}, f32[768,96]{0,1:T(8,128)}, u32[]{:S(2)}) copy-start(f32[768,96]{0,1:T(8,128)} %param.42) | copy-start | bytes 884740
  849.4 232.5 %copy-start.63 = (f32[768,96]{0,1:T(8,128)S(1)}, f32[768,96]{0,1:T(8,128)}, u32[]{:S(2)}) copy-start(f32[768,96]{0,1:T(8,128)} %param.41) | copy-start | bytes 884740
  (110 other events, 1023.3 us)
Sparse Core Ops, SparseCore 0:
  128.5 122.2 all-reduce.7
  290.5 119.7 all-reduce.9
  557.7 221.2 all-reduce.13
  783.2 237.2 all-reduce.11
where the time goes:
time: 1100 us; the launch traced here: 1090 us
  waiting for transfers between devices  586 us (53%)
  matrix products  205 us (19%)
  other arithmetic  164 us (15%)
  blocking collectives  80.9 us (7%)
  local copies, waits for them, and re-layouts  32 us (3%)
  between operations  24.3 us (2%)
    psum x1, waiting for transfers between devices, local(): lax.psum(jnp.dot(gated, down_low, preferred_element_type=jnp.float32), 'mp')  184 us
    psum x1, waiting for transfers between devices, local(): summed = lax.psum((grad_qkv, grad_outw, grad_up, grad_down), 'dp')  171 us
    psum x1, waiting for transfers between devices, local(): lax.psum(jnp.dot(mixed, out_low, preferred_element_type=jnp.float32), 'mp')  122 us
    psum x1, waiting for transfers between devices, local(): lax.psum(jnp.einsum('sf,df->sd', grad_upper, up_low, preferred_element_ty...  109 us
    psum x1, blocking collectives, local(): count, attn_total, mlp_total = lax.psum((count_here, attn_sq, mlp_sq), 'dp')  41.8 us
    psum x1, blocking collectives, local(): sq_total = lax.psum(raw_sq, ('dp', 'mp'))  39.1 us
    convert_element_type x4, other arithmetic, local(): grad_scores = (probs_full * (grad_probs - delta)).astype(jnp.bfloat16)  33.6 us
    dot_general x4, matrix products, local(): jnp.einsum('qhd,khd->hqk', grad_block, v_in, preferred_element_type=jnp.f...  32.5 us
  transfers between devices with their start and end apart: 4, of which 4 were waited for; matrix products, arithmetic and copies ran while one was open for 7% of the time, Pallas kernels for 0%

commit v1 on v0

v1 whole, which is shorter than its diff:
```python
import functools

import jax
import jax.numpy as jnp
from jax import lax
from jax.experimental import pallas as pl
from jax.experimental.pallas import tpu as pltpu
from jax.sharding import PartitionSpec as P

NORM_EPS = 1e-06
CLIP_LIMIT = 1.0
LEARN_RATE = 0.1
BETA_ONE = 0.9
BETA_TWO = 0.95
ADAM_EPS = 1e-08
WEIGHT_DECAY = 0.1
SEG_BOUND = 512
BLOCK = 256
LANES = 128
F32 = jnp.float32
BF16 = jnp.bfloat16


def adam_step(weight, grad, first, second, factor, corr_one, corr_two, decay):
    grad = factor * grad
    first = BETA_ONE * first + (1.0 - BETA_ONE) * grad
    second = BETA_TWO * second + (1.0 - BETA_TWO) * grad * grad
    update = first / corr_one / (jnp.sqrt(second / corr_two) + ADAM_EPS)
    return (weight - LEARN_RATE * (update + decay * weight), first, second)


def dot(left, right, left_dim, right_dim):
    return lax.dot_general(
        left, right, (((left_dim,), (right_dim,)), ((), ())), preferred_element_type=F32
    )


class Links:
    def __init__(self):
        self.dp_size = lax.axis_size("dp")
        self.mp_size = lax.axis_size("mp")
        self.bits = self.dp_size.bit_length() - 1
        self.dp = lax.axis_index("dp")
        self.mp = lax.axis_index("mp")

    def core(self, array):
        return lax.ppermute(array, "mp", [(i, i ^ 1) for i in range(self.mp_size)])

    def half(self, array):
        return lax.ppermute(array, "mp", [(i, i ^ 2) for i in range(self.mp_size)])

    def data(self, array, bit):
        return lax.ppermute(array, "dp", [(i, i ^ (1 << bit)) for i in range(self.dp_size)])

    def bit(self, bit):
        return (self.dp >> bit) & 1

    def sum_all(self, array):
        array = array + self.core(array)
        array = array + self.half(array)
        return self.sum_data(array)

    def sum_data(self, array):
        for bit in range(self.bits):
            array = array + self.data(array, bit)
        return array


def hold(value, *after):
    return lax.optimization_barrier((value, *after))[0]


def quarter_of(links, weight, axis):
    rows = weight.shape[axis] // 4
    return lax.dynamic_slice_in_dim(weight, (links.dp & 3) * rows, rows, axis)


def quarter_spots(links):
    return jnp.stack([(links.dp & 3) ^ change for change in range(4)])


class Reduction:
    def __init__(self, links, grad):
        self.links = links
        self.left = list(range(links.bits - 1, -1, -1))
        self.array = grad.reshape((2,) * links.bits + (grad.shape[0] >> links.bits, grad.shape[1]))

    def send(self, step):
        if step == "half":
            own = self.array.shape[-1] // 2
            self.kept = self.array[..., :own]
            return self.array[..., own:]
        axis = self.left.index(step)
        self.left.remove(step)
        mine = self.links.bit(step)
        self.kept = lax.dynamic_index_in_dim(self.array, mine, axis, keepdims=False)
        return lax.dynamic_index_in_dim(self.array, 1 - mine, axis, keepdims=False)

    def take(self, arrived):
        self.array = self.kept + arrived

    def step(self, step, *after):
        sent = self.send(step)
        sent = hold(sent, *after) if after else sent
        self.take(self.links.half(sent) if step == "half" else self.links.data(sent, step))


def vmem_specs(count):
    return [pl.BlockSpec(memory_space=pltpu.VMEM)] * count


def smem_specs(count):
    return [pl.BlockSpec(memory_space=pltpu.SMEM)] * count


def cost(flops, bytes_accessed, transcendentals=0):
    return pl.CostEstimate(
        flops=int(flops), bytes_accessed=int(bytes_accessed), transcendentals=int(transcendentals)
    )


def normed(values, axis):
    scale = 1.0 / values.shape[axis]
    center = values - jnp.sum(values, axis=axis, keepdims=True) * scale
    spread = jnp.sum(center * center, axis=axis, keepdims=True) * scale
    factor = lax.rsqrt(spread + NORM_EPS)
    return center * factor, factor


def normed_back(grad_hat, hat, factor, axis):
    scale = 1.0 / hat.shape[axis]
    mean = jnp.sum(grad_hat, axis=axis, keepdims=True) * scale
    along = jnp.sum(grad_hat * hat, axis=axis, keepdims=True) * scale
    return factor * (grad_hat - mean - hat * along)


def fold_rows(values):
    return jnp.sum(values.reshape(values.shape[0] // 8, 8, values.shape[1]), axis=0)


def fold_lanes(values):
    total = values[:, :LANES]
    for start in range(LANES, values.shape[1], LANES):
        total = total + values[:, start : start + LANES]
    return total


def column(row, count):
    return jnp.transpose(jnp.broadcast_to(row, (count, row.shape[1])))


def plan_kernel(window, half_ref, seg_ref, keep_ref, plan_ref, qseg_ref, kcode_ref, kept_ref):
    seq_len = seg_ref.shape[1]
    seg = seg_ref[...]
    half = half_ref[0]
    places = lax.broadcasted_iota(jnp.int32, (1, seq_len), 1)
    starts = (seg != pltpu.roll(seg, 1, 1)) & (places > 0)
    ranking = jnp.where(starts, jnp.abs(places - seq_len // 2) * (4 * seq_len) + places, 1 << 30)
    parting = lax.rem(jnp.min(ranking), 4 * seq_len)
    start = pl.multiple_of(half * (seq_len - window), LANES)
    low_valid = jnp.where(half == 0, 0, parting - start)
    high_valid = jnp.where(half == 0, parting, window)
    seg_win = seg_ref[:, pl.ds(start, window)]
    keep_win = keep_ref[:, pl.ds(start, window)]
    spots = lax.broadcasted_iota(jnp.int32, (1, window), 1)
    valid = (spots >= low_valid) & (spots < high_valid)
    qseg_ref[...] = jnp.broadcast_to(seg_win, (8, window))
    kcode_ref[...] = column(jnp.where(keep_win == 1, seg_win, -1), LANES)
    kept_ref[...] = column(jnp.where(valid & (keep_win == 1), 1.0, 0.0), LANES)
    segs = jnp.broadcast_to(seg_win, (8, window))
    lanes = lax.broadcasted_iota(jnp.int32, (8, window), 1)
    block = lax.broadcasted_iota(jnp.int32, (8, window), 0) * BLOCK

    def total(values):
        return jnp.sum(values, axis=1, keepdims=True)

    first_seg = total(jnp.where(lanes == block, segs, 0))
    last_seg = total(jnp.where(lanes == block + (BLOCK - 1), segs, 0))
    low = total(jnp.where(segs < first_seg, 1, 0))
    high = total(jnp.where(segs <= last_seg, 1, 0))
    block_first = block[:, :1]
    low = jnp.maximum(low, low_valid)
    high = jnp.minimum(high, high_valid) + (BLOCK - 1)
    shift = BLOCK.bit_length() - 1
    low, high = low >> shift, high >> shift
    live = (block_first < high_valid) & (block_first + BLOCK > low_valid)
    high = jnp.where(live, high, low)
    lane = lax.broadcasted_iota(jnp.int32, (8, LANES), 1)
    plan = jnp.where(lane == 0, low, jnp.where(lane == 1, high, parting))
    plan_ref[...] = plan


def make_plan(links, seg_row, keep_row, window):
    half = jnp.full((1,), links.mp // 2, jnp.int32)
    return pl.pallas_call(
        functools.partial(plan_kernel, window),
        out_shape=(
            jax.ShapeDtypeStruct((8, LANES), jnp.int32),
            jax.ShapeDtypeStruct((8, window), jnp.int32),
            jax.ShapeDtypeStruct((window, LANES), jnp.int32),
            jax.ShapeDtypeStruct((window, LANES), F32),
        ),
        in_specs=smem_specs(1) + vmem_specs(2),
        out_specs=tuple(vmem_specs(4)),
        cost_estimate=cost(0, window * 1100),
        name="plan_window",
    )(half, seg_row, keep_row)


def allowed_block(kcode_ref, qseg_ref, key_start, query_start):
    codes = kcode_ref[pl.ds(key_start, BLOCK), :]
    codes = jnp.concatenate([codes] * (BLOCK // LANES), axis=1)
    segs = qseg_ref[0:1, pl.ds(query_start, BLOCK)]
    rows = lax.broadcasted_iota(jnp.int32, (BLOCK, BLOCK), 0)
    cols = lax.broadcasted_iota(jnp.int32, (BLOCK, BLOCK), 1)
    return (codes == segs) | (rows - cols == query_start - key_start)


def project_heads(heads, dim, weight, a_ref, params_ref, qkv_refs, hat_refs, factor_ref):
    tokens = a_ref.shape[0]
    group = heads * dim

    def block(tb, carry):
        ts = pl.multiple_of(tb * BLOCK, BLOCK)
        here = pl.ds(ts, BLOCK)
        rows = a_ref[here, :]
        for which in range(3):
            raw = dot(weight[which][...], rows, 1, 1) + params_ref[:, which : which + 1]
            if which == 2:
                qkv_refs[2][:, here] = raw.astype(BF16)
                continue
            hat, factor = normed(raw.reshape(heads, dim, BLOCK), 1)
            hat = hat.reshape(group, BLOCK)
            gained = hat * params_ref[:, 3 + which : 4 + which]
            if which == 0:
                gained = gained * dim ** (-0.5)
            qkv_refs[which][:, here] = gained.astype(BF16)
            hat_refs[which][:, here] = hat.astype(BF16)
            for head in range(heads):
                spot = (which * heads + head) * 8
                factor_ref[pl.ds(spot, 8), here] = jnp.broadcast_to(factor[head], (8, BLOCK))
        return carry

    lax.fori_loop(0, tokens // BLOCK, block, 0)


def attend(heads, dim, plan_ref, q_ref, k_ref, v_ref, kcode_ref, qseg_ref, o_ref, inv_ref, acc, tot):
    tokens = q_ref.shape[1]

    def query_block(qb, carry):
        qs = pl.multiple_of(qb * BLOCK, BLOCK)
        acc[...] = jnp.zeros_like(acc)
        tot[...] = jnp.zeros_like(tot)

        def key_block(kb, carry):
            ks = pl.multiple_of(kb * BLOCK, BLOCK)
            allowed = allowed_block(kcode_ref, qseg_ref, ks, qs)
            for head in range(heads):
                rows = pl.ds(head * dim, dim)
                scores = dot(k_ref[rows, pl.ds(ks, BLOCK)], q_ref[rows, pl.ds(qs, BLOCK)], 0, 0)
                expo = jnp.where(allowed, jnp.exp(scores), 0.0)
                tot[pl.ds(head * 8, 8), :] += fold_rows(expo)
                acc[rows, :] += dot(v_ref[rows, pl.ds(ks, BLOCK)], expo.astype(BF16), 1, 0)
            return carry

        lax.fori_loop(plan_ref[qb, 0], plan_ref[qb, 1], key_block, 0)
        for head in range(heads):
            rows = pl.ds(head * dim, dim)
            total = jnp.sum(tot[pl.ds(head * 8, 8), :], axis=0, keepdims=True)
            inverse = jnp.where(total > 0.0, 1.0 / total, 0.0)
            o_ref[rows, pl.ds(qs, BLOCK)] = (acc[rows, :] * inverse).astype(BF16)
            inv_ref[pl.ds(head * 8, 8), pl.ds(qs, BLOCK)] = jnp.broadcast_to(inverse, (8, BLOCK))
        return carry

    lax.fori_loop(0, tokens // BLOCK, query_block, 0)


def own_heads_kernel(
    heads, dim, x_ref, vec_ref, weight_ref, params_ref,
    a_ref, q_ref, k_ref, v_ref, qh_ref, kh_ref, factor_ref, weight,
):
    weight[...] = weight_ref[...].astype(BF16)
    tokens = x_ref.shape[0]

    def norm_block(tb, carry):
        here = pl.ds(pl.multiple_of(tb * BLOCK, BLOCK), BLOCK)
        hat, _ = normed(x_ref[here, :].astype(F32), 1)
        a_ref[here, :] = (hat * vec_ref[0:1, :] + vec_ref[1:2, :]).astype(BF16)
        return carry

    lax.fori_loop(0, tokens // BLOCK, norm_block, 0)
    project_heads(
        heads, dim, [weight.at[k] for k in range(3)], a_ref, params_ref, (q_ref, k_ref, v_ref),
        (qh_ref, kh_ref), factor_ref,
    )


def other_heads_kernel(
    heads, dim, spots_ref, a_ref, own_ref, p0, p1, p2, p3, params_ref,
    q_ref, k_ref, v_ref, qh_ref, kh_ref, factor_ref, qk_ref, value_ref,
):
    group = heads * dim
    places = [
        (qk_ref.at[pl.ds(0, group)], qk_ref.at[pl.ds(2 * group, group)]),
        (qk_ref.at[pl.ds(group, group)], qk_ref.at[pl.ds(3 * group, group)]),
        (value_ref.at[pl.ds(0, group)], value_ref.at[pl.ds(group, group)]),
    ]
    for which, (own_place, place) in enumerate(places):
        own_place[...] = own_ref[which].astype(BF16)
        for index, piece in enumerate((p0, p1, p2, p3)):
            count = piece.shape[1]
            spot = pl.multiple_of(spots_ref[index] * count, 16)
            place[pl.ds(spot, count), :] = piece[which].astype(BF16)
    project_heads(
        heads, dim, [place for _, place in places], a_ref, params_ref, (q_ref, k_ref, v_ref), (qh_ref, kh_ref), factor_ref
    )


def attention_kernel(
    heads, dim, plan_ref, q_ref, k_ref, v_ref, kcode_ref, qseg_ref, o_ref, inv_ref, acc, tot
):
    attend(heads, dim, plan_ref, q_ref, k_ref, v_ref, kcode_ref, qseg_ref, o_ref, inv_ref, acc, tot)


def out_kernel(o_own_ref, o_other_ref, own_ref, other_ref, part_ref, weight, o_cat):
    group = own_ref.shape[0]

    @pl.when(pl.program_id(0) == 0)
    def _():
        weight[pl.ds(0, group), :] = own_ref[...].astype(BF16)
        weight[pl.ds(group, group), :] = other_ref[...].astype(BF16)

    o_cat[pl.ds(0, group), :] = o_own_ref[...]
    o_cat[pl.ds(group, group), :] = o_other_ref[...]
    part_ref[...] = dot(o_cat[...], weight[...], 0, 0)


def head_shapes(group, heads, tokens):
    narrow = jax.ShapeDtypeStruct((group, tokens), BF16)
    return [*(narrow,) * 5, jax.ShapeDtypeStruct((heads * 16, tokens), F32)]


def o_shapes(group, heads, tokens):
    return [
        jax.ShapeDtypeStruct((group, tokens), BF16),
        jax.ShapeDtypeStruct((heads * 8, tokens), F32),
    ]


def own_heads(x_win, vec_params, weight, params, heads, dim):
    tokens, width = x_win.shape
    group = heads * dim
    return pl.pallas_call(
        functools.partial(own_heads_kernel, heads, dim),
        out_shape=[
            jax.ShapeDtypeStruct((tokens, width), BF16),
            *head_shapes(group, heads, tokens),
        ],
        in_specs=vmem_specs(4),
        out_specs=vmem_specs(7),
        scratch_shapes=[pltpu.VMEM((3, group, width), BF16)],
        cost_estimate=cost(tokens * width * group * 6, tokens * width * 8),
        name="heads_own",
    )(x_win, vec_params, weight, params)


def other_heads(spots, a_first, own_weight, pieces, params, heads, dim):
    tokens, width = a_first.shape
    group = heads * dim
    return pl.pallas_call(
        functools.partial(other_heads_kernel, heads, dim),
        out_shape=[
            *head_shapes(group, heads, tokens),
            jax.ShapeDtypeStruct((4 * group, width), BF16),
            jax.ShapeDtypeStruct((2 * group, width), BF16),
        ],
        in_specs=smem_specs(1) + vmem_specs(7),
        out_specs=vmem_specs(8),
        cost_estimate=cost(tokens * width * group * 6, tokens * width * 8),
        name="heads_other",
    )(spots, a_first, own_weight, *pieces, params)


def attention(plan, query, key, value, kcode, qseg, heads, dim):
    group, tokens = query.shape
    pairs = heads * tokens * 3 * BLOCK
    return pl.pallas_call(
        functools.partial(attention_kernel, heads, dim),
        out_shape=o_shapes(group, heads, tokens),
        in_specs=smem_specs(1) + vmem_specs(5),
        out_specs=vmem_specs(2),
        scratch_shapes=[pltpu.VMEM((group, BLOCK), F32), pltpu.VMEM((heads * 8, BLOCK), F32)],
        cost_estimate=cost(pairs * dim * 4, group * tokens * 8, pairs),
        name="attention",
    )(plan, query, key, value, kcode, qseg)


def out_project(o_own, o_other, out_own, out_other):
    group, tokens = o_own.shape
    width = out_own.shape[1]
    cols = pl.BlockSpec((group, BLOCK), lambda i: (0, i))
    return pl.pallas_call(
        out_kernel,
        grid=(tokens // BLOCK,),
        out_shape=jax.ShapeDtypeStruct((tokens, width), F32),
        in_specs=[cols, cols, whole_spec(out_own.shape), whole_spec(out_other.shape)],
        out_specs=rows_spec(width),
        scratch_shapes=[
            pltpu.VMEM((2 * group, width), BF16),
            pltpu.VMEM((2 * group, BLOCK), BF16),
        ],
        cost_estimate=cost(tokens * width * group * 4, tokens * width * 6),
        name="out_project",
    )(o_own, o_other, out_own, out_other)


def attention_back_kernel(
    heads, dim, plan_ref, q_ref, k_ref, v_ref, qh_ref, kh_ref, factor_ref, o_ref, inv_ref, do_ref,
    params_ref, kcode_ref, qseg_ref, *rest,
):
    draw_qk_ref, draw_v_ref = rest[-7:-5]
    out_sums_ref, dq_ref, dk_ref, dv_ref, sums_ref = rest[-5:]
    group, tokens = q_ref.shape
    for ref in (dq_ref, dk_ref, dv_ref, sums_ref):
        ref[...] = jnp.zeros_like(ref)

    def query_block(qb, carry):
        qs = pl.multiple_of(qb * BLOCK, BLOCK)
        here = pl.ds(qs, BLOCK)
        deltas = []
        inverses = []
        for head in range(heads):
            rows = pl.ds(head * dim, dim)
            products = do_ref[rows, here].astype(F32) * o_ref[rows, here].astype(F32)
            deltas.append(jnp.sum(products, axis=0, keepdims=True))
            inverses.append(inv_ref[pl.ds(head * 8, 1), here])

        def key_block(kb, carry):
            ks = pl.multiple_of(kb * BLOCK, BLOCK)
            there = pl.ds(ks, BLOCK)
            allowed = allowed_block(kcode_ref, qseg_ref, ks, qs)
            for head in range(heads):
                rows = pl.ds(head * dim, dim)
                query, key = q_ref[rows, here], k_ref[rows, there]
                grad_o = do_ref[rows, here]
                scores = dot(key, query, 0, 0)
                probs = jnp.where(allowed, jnp.exp(scores), 0.0) * inverses[head]
                grad_probs = dot(v_ref[rows, there], grad_o, 0, 0)
                grad_scores = (probs * (grad_probs - deltas[head])).astype(BF16)
                dv_ref[rows, there] += dot(grad_o, probs.astype(BF16), 1, 1)
                dk_ref[rows, there] += dot(query, grad_scores, 1, 1)
                dq_ref[rows, here] += dot(key, grad_scores, 1, 0)
            return carry

        lax.fori_loop(plan_ref[qb, 0], plan_ref[qb, 1], key_block, 0)
        return carry

    lax.fori_loop(0, tokens // BLOCK, query_block, 0)

    def token_block(tb, carry):
        here = pl.ds(pl.multiple_of(tb * BLOCK, BLOCK), BLOCK)
        for which, (grad_ref, hat_ref) in enumerate(((dq_ref, qh_ref), (dk_ref, kh_ref), (dv_ref, None))):
            rows = pl.ds(which * group, group)
            grad = grad_ref[:, here]
            if hat_ref is not None:
                if which == 0:
                    grad = grad * dim ** (-0.5)
                hat = hat_ref[:, here].astype(F32)
                sums_ref[pl.ds((3 + which) * group, group), :] += fold_lanes(grad * hat)
                grad = grad * params_ref[:, 3 + which : 4 + which]
                parts = []
                for head in range(heads):
                    lines = slice(head * dim, (head + 1) * dim)
                    factor = factor_ref[pl.ds((which * heads + head) * 8, 1), here]
                    parts.append(normed_back(grad[lines], hat[lines], factor, 0))
                grad = jnp.concatenate(parts, axis=0)
            rounded = grad.astype(BF16)
            if which < 2:
                draw_qk_ref[rows, here] = rounded
            else:
                draw_v_ref[:, here] = rounded
            sums_ref[rows, :] += fold_lanes(rounded.astype(F32))
        return carry

    lax.fori_loop(0, tokens // BLOCK, token_block, 0)
    out_sums_ref[...] = jnp.sum(jnp.transpose(sums_ref[...]), axis=0, keepdims=True)


def attention_back(plan, saved, grad_o, params, kcode, qseg, heads, dim, draws=None):
    group, tokens = saved[0].shape
    pairs = heads * tokens * 3 * BLOCK
    which = 0 if draws is None else 1
    sums = -(-5 * group // LANES) * LANES
    inputs = [*saved, grad_o, params, kcode, qseg]
    in_specs = smem_specs(1) + [whole_spec(x.shape) for x in inputs]
    aliases = {}
    if draws is not None:
        aliases = {1 + len(inputs) + k: k for k in range(2)}
        inputs += draws
        in_specs += [pl.BlockSpec(memory_space=pl.ANY)] * 2
    return pl.pallas_call(
        functools.partial(attention_back_kernel, heads, dim),
        grid=(1,),
        out_shape=[
            jax.ShapeDtypeStruct((4 * group, tokens), BF16),
            jax.ShapeDtypeStruct((2 * group, tokens), BF16),
            jax.ShapeDtypeStruct((1, sums), F32),
        ],
        in_specs=in_specs,
        out_specs=[
            pl.BlockSpec((2 * group, tokens), lambda i: (which, 0)),
            pl.BlockSpec((group, tokens), lambda i: (which, 0)),
            whole_spec((1, sums)),
        ],
        scratch_shapes=[
            *(pltpu.VMEM((group, tokens), F32),) * 3,
            pltpu.VMEM((sums, LANES), F32),
        ],
        input_output_aliases=aliases,
        cost_estimate=cost(pairs * dim * 10, group * tokens * 30, pairs),
        name="attention_back",
    )(plan, *inputs)


ERFC_TERMS = (
    0.16918800576031592, 0.17071521752915575, 0.14833923939584578, 0.2149257797248009,
    -0.09465005158893602, 0.5477190245253036, -0.5122771874066157, 0.4855627631921905,
    -0.1295228107166713,
)


def gelu_and_slope(values):
    t = 1.0 / (1.0 + (0.3 * 0.5**0.5) * jnp.abs(values))
    poly = ERFC_TERMS[-1]
    for term in ERFC_TERMS[-2::-1]:
        poly = poly * t + term
    bell = jnp.exp(values * values * -0.5)
    low_tail = 0.5 * (t * poly) * bell
    below = jnp.where(values > 0.0, 1.0 - low_tail, low_tail)
    return values * below, below + values * bell * 0.3989422804014327


def mlp_half(a, dmlp, up, down, bias):
    upper = dot(a, up, 1, 0) + bias
    gated, slope = gelu_and_slope(upper)
    gated = gated.astype(BF16)
    grad_gated = dot(dmlp, down, 1, 1)
    grad_upper = (grad_gated * slope).astype(BF16)
    return gated, grad_upper, dot(gated, down, 1, 0), dot(grad_upper, up, 1, 1)


def own_mlp_kernel(
    x_ref, mine_ref, peer_ref, cot_ref, kept_ref, vec_ref, up_ref, down_ref, bias_ref,
    hidden_ref, a_ref, dmlp_ref, g_ref, du_ref, mlp_ref, da_ref, bias_out, attn_out, up, down, bias_sums, attn_sums,
):
    @pl.when(pl.program_id(0) == 0)
    def _():
        up[...] = up_ref[...].astype(BF16)
        down[...] = down_ref[...].astype(BF16)
        bias_sums[...] = jnp.zeros_like(bias_sums)
        attn_sums[...] = jnp.zeros_like(attn_sums)

    kept = kept_ref[:, 0:1]
    attn = mine_ref[...] + peer_ref[...] + vec_ref[4:5, :]
    attn_sums[...] += fold_rows(kept * attn * attn)
    hidden = x_ref[...].astype(F32) + attn
    hidden_ref[...] = hidden
    hat, _ = normed(hidden, 1)
    a = (hat * vec_ref[2:3, :] + vec_ref[3:4, :]).astype(BF16)
    a_ref[...] = a
    dmlp = (cot_ref[...].astype(F32) * kept).astype(BF16)
    dmlp_ref[...] = dmlp
    gated, grad_upper, mlp, da = mlp_half(a, dmlp, up[...], down[...], bias_ref[...])
    g_ref[...] = gated
    du_ref[...] = grad_upper
    mlp_ref[...] = mlp
    da_ref[...] = da
    bias_sums[...] += fold_rows(grad_upper.astype(F32))

    @pl.when(pl.program_id(0) == pl.num_programs(0) - 1)
    def _():
        bias_out[...] = jnp.sum(bias_sums[...], axis=0, keepdims=True)
        attn_out[...] = jnp.sum(attn_sums[...], axis=0, keepdims=True)


def other_mlp_kernel(
    spots_ref, a_ref, dmlp_ref, mlp_in_ref, da_in_ref, base, near_a, near_b, far_a, far_b, bias_ref, g_in, du_in,
    g_ref, du_ref, mlp_ref, da_ref, bias_out, up, down, bias_sums,
):
    @pl.when(pl.program_id(0) == 0)
    def _():
        count = near_a.shape[1]
        for change, first, second in (
            (0, base.at[:, pl.ds(0, count)], base.at[:, pl.ds(count, count)]),
            (1, near_a, far_b.at[0]),
            (2, far_a.at[0], near_b),
            (3, far_a.at[1], far_b.at[1]),
        ):
            for which, piece in enumerate((first, second)):
                spot = pl.multiple_of((spots_ref[change] * 2 + which) * count, 16)
                up[pl.ds(spot, count), :] = piece[0].astype(BF16)
                down[pl.ds(spot, count), :] = piece[1].astype(BF16)
        bias_sums[...] = jnp.zeros_like(bias_sums)

    gated, grad_upper, mlp, da = mlp_half(
        a_ref[...], dmlp_ref[...], up[...], down[...], bias_ref[...]
    )
    g_ref[...] = gated
    du_ref[...] = grad_upper
    mlp_ref[...] = mlp_in_ref[...] + mlp
    da_ref[...] = da_in_ref[...] + da
    bias_sums[...] += fold_rows(grad_upper.astype(F32))

    @pl.when(pl.program_id(0) == pl.num_programs(0) - 1)
    def _():
        bias_out[...] = jnp.sum(bias_sums[...], axis=0, keepdims=True)


def rows_spec(width):
    return pl.BlockSpec((BLOCK, width), lambda i: (i, 0))


def whole_spec(shape):
    return pl.BlockSpec(shape, lambda *_: (0,) * len(shape), pipeline_mode=pl.Buffered(1))


def sums_spec(rows, width):
    return pl.BlockSpec((rows, width), lambda *_: (0, 0))


def own_mlp(x_win, mine, peer, cot, kept, vec_params, up_weight, down_weight, bias):
    tokens, width = x_win.shape
    units = up_weight.shape[1]
    wide = rows_spec(width)
    struct = jax.ShapeDtypeStruct
    return pl.pallas_call(
        own_mlp_kernel,
        grid=(tokens // BLOCK,),
        out_shape=[
            struct((tokens, width), F32),
            struct((tokens, width), BF16),
            struct((tokens, width), BF16),
            struct((tokens, 2 * units), BF16),
            struct((tokens, 2 * units), BF16),
            struct((tokens, width), F32),
            struct((tokens, width), F32),
            struct((1, units), F32),
            struct((1, width), F32),
        ],
        in_specs=[
            wide, wide, wide, wide, rows_spec(LANES), whole_spec(vec_params.shape),
            whole_spec(up_weight.shape), whole_spec(down_weight.shape), whole_spec(bias.shape),
        ],
        out_specs=[
            wide, wide, wide, rows_spec(units), rows_spec(units), wide, wide,
            sums_spec(1, units), sums_spec(1, width),
        ],
        scratch_shapes=[
            pltpu.VMEM(up_weight.shape, BF16),
            pltpu.VMEM(down_weight.shape, BF16),
            pltpu.VMEM((8, units), F32),
            pltpu.VMEM((8, width), F32),
        ],
        cost_estimate=cost(8 * tokens * width * units, tokens * width * 40, tokens * units * 2),
        name="mlp_own",
    )(x_win, mine, peer, cot, kept, vec_params, up_weight, down_weight, bias)


def other_mlp(spots, a_second, dmlp, mlp_part, da_part, pieces, bias, activations):
    tokens, width = a_second.shape
    units = bias.shape[1]
    wide = rows_spec(width)
    later = pl.BlockSpec((BLOCK, units), lambda i: (i, 1))
    struct = jax.ShapeDtypeStruct
    return pl.pallas_call(
        other_mlp_kernel,
        grid=(tokens // BLOCK,),
        out_shape=[
            struct((tokens, 2 * units), BF16),
            struct((tokens, 2 * units), BF16),
            struct((tokens, width), F32),
            struct((tokens, width), F32),
            struct((1, units), F32),
        ],
        in_specs=[
            *smem_specs(1), wide, wide, wide, wide,
            *(whole_spec(piece.shape) for piece in pieces), whole_spec(bias.shape),
            *(pl.BlockSpec(memory_space=pl.ANY),) * 2,
        ],
        out_specs=[later, later, wide, wide, sums_spec(1, units)],
        input_output_aliases={3: 2, 4: 3, 6 + len(pieces): 0, 7 + len(pieces): 1},
        scratch_shapes=[
            pltpu.VMEM((width, units), BF16),
            pltpu.VMEM((units, width), BF16),
            pltpu.VMEM((8, units), F32),
        ],
        cost_estimate=cost(8 * tokens * width * units, tokens * width * 28, tokens * units * 2),
        name="mlp_other",
    )(spots, a_second, dmlp, mlp_part, da_part, *pieces, bias, *activations)


def hidden_back_kernel(
    group, hidden_ref, mine_ref, peer_ref, cot_ref, kept_ref, vec_ref, out_own_ref, out_other_ref,
    dh_ref, dattn_ref, do_own_ref, do_other_ref, sums_out, out_weight, sums_ref,
):
    @pl.when(pl.program_id(0) == 0)
    def _():
        out_weight[pl.ds(0, group), :] = out_own_ref[...].astype(BF16)
        out_weight[pl.ds(group, group), :] = out_other_ref[...].astype(BF16)
        sums_ref[...] = jnp.zeros_like(sums_ref)

    hat, factor = normed(hidden_ref[...], 1)
    da = mine_ref[...] + peer_ref[...]
    dy = cot_ref[...].astype(F32) * kept_ref[:, 0:1]
    dh = dy + normed_back(da * vec_ref[2:3, :], hat, factor, 1)
    dh_ref[...] = dh
    dattn = dh.astype(BF16)
    dattn_ref[...] = dattn
    grads = dot(out_weight[...], dattn, 1, 1).astype(BF16)
    do_own_ref[...] = grads[:group]
    do_other_ref[...] = grads[group:]
    sums_ref[0:8, :] += fold_rows(da * hat)
    sums_ref[8:16, :] += fold_rows(da)
    sums_ref[16:24, :] += fold_rows(dattn.astype(F32))
    sums_ref[24:32, :] += fold_rows(dy.astype(BF16).astype(F32))

    @pl.when(pl.program_id(0) == pl.num_programs(0) - 1)
    def _():
        for row in range(4):
            total = jnp.sum(sums_ref[8 * row : 8 * row + 8, :], axis=0, keepdims=True)
            sums_out[row : row + 1, :] = total


def hidden_back(hidden, mine, peer, cot, kept, vec_params, out_own, out_other):
    tokens, width = hidden.shape
    group = out_own.shape[0]
    wide = rows_spec(width)
    cols = pl.BlockSpec((group, BLOCK), lambda i: (0, i))
    struct = jax.ShapeDtypeStruct
    return pl.pallas_call(
        functools.partial(hidden_back_kernel, group),
        grid=(tokens // BLOCK,),
        out_shape=[
            struct((tokens, width), F32),
            struct((tokens, width), BF16),
            struct((group, tokens), BF16),
            struct((group, tokens), BF16),
            struct((4, width), F32),
        ],
        in_specs=[
            wide, wide, wide, wide, rows_spec(LANES), whole_spec(vec_params.shape),
            whole_spec(out_own.shape), whole_spec(out_other.shape),
        ],
        out_specs=[wide, wide, cols, cols, sums_spec(4, width)],
        scratch_shapes=[pltpu.VMEM((2 * group, width), BF16), pltpu.VMEM((32, width), F32)],
        cost_estimate=cost(4 * tokens * width * group, tokens * width * 22),
        name="hidden_back",
    )(hidden, mine, peer, cot, kept, vec_params, out_own, out_other)


def input_back_kernel(
    core_ref, mine_ref, peer_ref, x_ref, dh_ref, vec_ref, out_ref, sums_out, sums_ref
):
    @pl.when(pl.program_id(0) == 0)
    def _():
        sums_ref[...] = jnp.zeros_like(sums_ref)

    hat, factor = normed(x_ref[...].astype(F32), 1)
    da = mine_ref[...] + peer_ref[...]
    out_ref[...] = dh_ref[...] + normed_back(da * vec_ref[0:1, :], hat, factor, 1)
    sums_ref[0:8, :] += fold_rows(da * hat)
    sums_ref[8:16, :] += fold_rows(da)

    @pl.when(pl.program_id(0) == pl.num_programs(0) - 1)
    def _():
        for row in range(2):
            total = jnp.sum(sums_ref[8 * row : 8 * row + 8, :], axis=0, keepdims=True)
            sums_out[row : row + 1, :] = total


def input_back(core, mine, peer, x_win, dh, vec_params):
    half_rows, width = peer.shape
    step = LANES
    count = half_rows // step
    near = pl.BlockSpec((step, width), lambda i, core_ref: (i, 0))
    window = pl.BlockSpec((step, width), lambda i, core_ref: (core_ref[0] * count + i, 0))
    struct = jax.ShapeDtypeStruct
    return pl.pallas_call(
        input_back_kernel,
        grid_spec=pltpu.PrefetchScalarGridSpec(
            num_scalar_prefetch=1,
            grid=(count,),
            in_specs=[window, near, window, window, whole_spec(vec_params.shape)],
            out_specs=[near, sums_spec(2, width)],
            scratch_shapes=[pltpu.VMEM((16, width), F32)],
        ),
        out_shape=[struct((half_rows, width), F32), struct((2, width), F32)],
        cost_estimate=cost(0, half_rows * width * 18),
        name="input_back",
    )(core, mine, peer, x_win, dh, vec_params)


def join_kernel(half_rows, window, info_ref, factor_ref, shift_ref, mine_ref, near_ref, far_ref, far_near_ref, out_ref):
    seq_len = out_ref.shape[1]
    core, half, parting = info_ref[0], info_ref[1], info_ref[2]
    factor = factor_ref[0]
    step = LANES

    def rows_of(which, row):
        from_core = row // half_rows
        spot = pl.ds(row % half_rows, step)
        own = half == which
        same = core == from_core
        return jnp.where(
            own,
            jnp.where(same, mine_ref[spot, :], near_ref[spot, :]),
            jnp.where(same, far_ref[spot, :], far_near_ref[spot, :]),
        )

    offset = seq_len - window
    for row in range(0, seq_len, step):
        if row + step <= offset:
            values = rows_of(0, row)
        elif row >= window:
            values = rows_of(1, row - offset)
        else:
            places = row + lax.broadcasted_iota(jnp.int32, (step, 1), 0)
            values = jnp.where(places < parting, rows_of(0, row), rows_of(1, row - offset))
        out_ref[0, pl.ds(row, step), :] = (values * factor + shift_ref[...]).astype(BF16)


def join_sequence(links, mine, near, far, far_near, parting, seq_len, window, factor, shift):
    half_rows, width = mine.shape
    info = jnp.stack([links.mp % 2, links.mp // 2, parting]).astype(jnp.int32)
    return pl.pallas_call(
        functools.partial(join_kernel, half_rows, window),
        out_shape=jax.ShapeDtypeStruct((1, seq_len, width), BF16),
        in_specs=smem_specs(2) + vmem_specs(5),
        out_specs=pl.BlockSpec(memory_space=pltpu.VMEM),
        cost_estimate=cost(0, half_rows * width * 16 + seq_len * width * 2),
        name="join_sequence",
    )(info, factor, shift, mine, near, far, far_near)


def last_gradients_kernel(
    group, a_ref, dattn_ref, qk_ref, v_ref, o_own_ref, o_other_ref, qk_own_out, qk_other_out, vo_out
):
    a, dattn = a_ref[...], dattn_ref[...]
    query_key = jnp.transpose(dot(qk_ref[...], a, 1, 0))
    qk_own_out[...] = query_key[:, : 2 * group]
    qk_other_out[...] = query_key[:, 2 * group :]
    value = dot(v_ref[...], a, 1, 0)
    own, other = dot(o_own_ref[...], dattn, 1, 0), dot(o_other_ref[...], dattn, 1, 0)
    rows = jnp.concatenate([value[:group], own, value[group:], other], axis=0)
    vo_out[...] = jnp.transpose(rows)


def last_gradients(a_first, dattn, draw_qk, draw_v, o_own, o_other):
    tokens, width = a_first.shape
    group = o_own.shape[0]
    cols = pl.BlockSpec((tokens, BLOCK), lambda i: (0, i))
    narrow, wide = rows_spec(2 * group), rows_spec(4 * group)
    struct = jax.ShapeDtypeStruct
    inputs = (draw_qk, draw_v, o_own, o_other)
    return pl.pallas_call(
        functools.partial(last_gradients_kernel, group),
        grid=(width // BLOCK,),
        out_shape=[
            struct((width, 2 * group), F32),
            struct((width, 2 * group), F32),
            struct((width, 4 * group), F32),
        ],
        in_specs=[cols, cols, *(whole_spec(x.shape) for x in inputs)],
        out_specs=[narrow, narrow, wide],
        cost_estimate=cost(16 * tokens * width * group, tokens * width * 12),
        name="last_gradients",
    )(a_first, dattn, *inputs)


def pack_kernel(
    core_ref, first_ref, second_ref, kept_ref, attn_ref, mlp_ref,
    own_ref, other_ref, own_bias_ref, other_bias_ref, mine_ref, away_ref,
):
    width = mine_ref.shape[1]
    once = jnp.where(core_ref[0] == 0, 1.0, 0.0)
    count = jnp.sum(kept_ref[...]) * (once / kept_ref.shape[1])
    attn = jnp.sum(attn_ref[...]) * once
    lane = lax.broadcasted_iota(jnp.int32, (1, width), 1)
    stats = jnp.where(lane == 0, count, jnp.where(lane == 1, attn, jnp.where(lane == 2, mlp_ref[0], 0.0)))
    sums, units = own_ref.shape[1], own_bias_ref.shape[1]
    for ref, head, bias in ((mine_ref, own_ref, own_bias_ref), (away_ref, other_ref, other_bias_ref)):
        ref[...] = jnp.zeros_like(ref)
        ref[0:2, :] = first_ref[...]
        ref[2:6, :] = second_ref[...] * once
        ref[6:7, :] = stats
        row = 8
        for source, size in ((head, sums), (bias, units)):
            for start in range(0, size, width):
                length = min(width, size - start)
                ref[row : row + 1, :length] = source[:, start : start + length]
                row += 1


def pack_small(core, first, second, kept, attn, mlp_sq, own, other, own_bias, other_bias):
    width = first.shape[1]
    inputs = (first, second, kept, attn)
    more = (own, other, own_bias, other_bias)
    rows = 8 + -(-own.shape[1] // width) + -(-own_bias.shape[1] // width)
    struct = jax.ShapeDtypeStruct((-(-rows // 8) * 8, width), F32)
    return pl.pallas_call(
        pack_kernel,
        out_shape=[struct, struct],
        in_specs=smem_specs(1) + vmem_specs(4) + smem_specs(1) + vmem_specs(4),
        out_specs=vmem_specs(2),
        cost_estimate=cost(0, kept.size * 4),
        name="pack_small",
    )(core, *inputs, mlp_sq, *more)


def update_kernel(decays, *refs):
    scalars, count = refs[0], len(decays)
    inputs, outputs = refs[1 : 1 + 4 * count], refs[1 + 4 * count :]
    factor, corr_one, corr_two = scalars[0], scalars[1], scalars[2]
    for index, decay in enumerate(decays):
        weight, grad, first, second = (ref[...] for ref in inputs[4 * index : 4 * index + 4])
        results = adam_step(weight, grad, first, second, factor, corr_one, corr_two, decay)
        for ref, value in zip(outputs[3 * index : 3 * index + 3], results):
            ref[...] = value


def update(scalars, groups, decays):
    inputs = [array for group in groups for array in group]
    shapes = [
        jax.ShapeDtypeStruct(group[0].shape, F32) for group in groups for _ in range(3)
    ]
    results = pl.pallas_call(
        functools.partial(update_kernel, decays),
        out_shape=shapes,
        in_specs=smem_specs(1) + vmem_specs(len(inputs)),
        out_specs=vmem_specs(len(shapes)),
        cost_estimate=cost(0, sum(28 * group[0].size for group in groups)),
        name="update",
    )(scalars, *inputs)
    return [results[3 * k : 3 * k + 3] for k in range(len(groups))]


def local(
    patches, cotangent, keep_mask, segment_ids, step_count,
    qkv_weight, qkv_first, qkv_second,
    out_weight, out_first, out_second,
    up_weight, up_first, up_second,
    down_weight, down_first, down_second,
    head_params, head_first, head_second,
    up_bias, upb_first, upb_second,
    vec_params, vec_first, vec_second,
):
    links = Links()
    seq_len, width = patches.shape[1:]
    heads, dim = head_params.shape[1:]
    group = heads * dim
    units = up_weight.shape[1]
    window = seq_len // 2 + SEG_BOUND // 2
    half_rows = window // 2
    core = links.mp % 2
    start = (links.mp // 2) * (seq_len - window)

    qkv_flip = jnp.swapaxes(qkv_weight, 1, 2)
    qkv_base = links.half(quarter_of(links, qkv_flip, 1))
    small = jnp.concatenate([head_params.reshape(-1), up_bias])
    small_other = links.half(small)
    head_other = small_other[: head_params.size].reshape(head_params.shape)

    def columns(params):
        return jnp.pad(params.reshape(params.shape[0], group).T, ((0, 0), (0, 3)))

    head_cols = columns(head_params)
    other_cols = columns(head_other)
    upb_own = up_bias.reshape(1, units)
    upb_other = small_other[head_params.size :].reshape(1, units)

    plan, qseg, kcode, kept = make_plan(links, segment_ids, keep_mask, window)
    parting = plan[0, 2]
    x_win = lax.dynamic_slice_in_dim(patches[0], start, window, 0)
    cot_win = lax.dynamic_slice_in_dim(cotangent[0], start, window, 0)
    a_first, *own = own_heads(x_win, vec_params, qkv_flip, head_cols, heads, dim)

    qkv_base = hold(qkv_base, own[0])
    qkv_pieces = [qkv_base, links.data(qkv_base, 0), links.data(qkv_base, 1)]
    both = [(i, i ^ 3) for i in range(links.dp_size)]
    qkv_pieces.append(lax.ppermute(qkv_base, "dp", both))
    spots = quarter_spots(links)
    up_down = quarter_of(links, jnp.stack([up_weight, down_weight]), 1)
    mlp_base = links.half(hold(up_down, qkv_base, small_other))
    own += attention(plan, hold(own[0], qkv_base), own[1], own[2], kcode, qseg, heads, dim)

    qkv_pieces = list(lax.optimization_barrier((*qkv_pieces, own[6]))[:4])
    *other, qk_cat, value_cat = other_heads(
        spots, a_first, qkv_flip, qkv_pieces, other_cols, heads, dim
    )
    mlp_base = hold(mlp_base, other[0])
    out_other = links.half(hold(out_weight, own[6]))
    eighth = mlp_base.shape[1] // 2
    part_a, part_b = mlp_base[:, :eighth], mlp_base[:, eighth:]
    near_a, near_b = links.data(part_a, 0), links.data(part_b, 1)
    other += attention(plan, hold(other[0], mlp_base), other[1], other[2], kcode, qseg, heads, dim)
    o_other, near_a, near_b = lax.optimization_barrier((other[6], near_a, near_b))
    attn_part = out_project(own[6], o_other, out_weight, out_other)
    pair_a, pair_b = jnp.stack([part_a, near_a]), jnp.stack([part_b, near_b])
    far_a, far_b = links.data(pair_a, 1), links.data(pair_b, 0)
    attn_peer = links.core(attn_part)
    hidden, a_second, dmlp, gated, grad_upper, mlp_part, da_part, upb_sums, attn_sums = own_mlp(
        x_win, attn_part, attn_peer, cot_win, kept, vec_params, up_weight, down_weight, upb_own
    )
    gated, grad_upper, mlp_part, da_part, upb_sums_other = other_mlp(
        spots, a_second, dmlp, mlp_part, da_part, (mlp_base, near_a, near_b, far_a, far_b), upb_other,
        (gated, grad_upper),
    )
    da_peer = links.core(da_part)
    down = Reduction(links, dot(dmlp, gated, 0, 0))
    up = Reduction(links, dot(a_second, grad_upper, 0, 0))
    down_sent, up_sent = down.send(0), up.send(1)
    down_got, up_got = links.data(down_sent, 0), links.data(up_sent, 1)
    dh, dattn, do_own, do_other, row_sums = hidden_back(
        hold(hidden, down_sent, up_sent), da_part, da_peer, cot_win, kept, vec_params,
        out_weight, out_other,
    )

    def my_rows(array):
        return lax.dynamic_slice_in_dim(array, core * half_rows, half_rows, 0)

    def peer_rows(array):
        return lax.dynamic_slice_in_dim(array, (1 - core) * half_rows, half_rows, 0)

    mlp_sum = my_rows(mlp_part) + links.core(peer_rows(mlp_part))
    result_mine = my_rows(hidden) + mlp_sum
    result_far, result_near = links.half(result_mine), links.core(result_mine)
    mlp_mine = mlp_sum + vec_params[5]
    mlp_sq = jnp.sum(my_rows(kept[:, :1]) * mlp_mine * mlp_mine)
    *draws, own_sums = attention_back(
        plan, own, hold(do_own, result_mine), head_cols, kcode, qseg, heads, dim
    )
    down.take(hold(down_got, draws[1]))
    up.take(hold(up_got, draws[1]))
    down_sent, up_sent = down.send("half"), up.send(0)
    down_got, up_got = links.half(down_sent), links.data(up_sent, 0)
    *draws, other_sums = attention_back(
        plan, other, hold(do_other, down_sent, up_sent, result_far, result_near), other_cols, kcode,
        qseg, heads, dim, draws,
    )
    result_far_near = links.core(result_far)
    down.take(hold(down_got, draws[1]))
    up.take(hold(up_got, draws[1]))
    down_sent, up_sent = down.send(1), up.send("half")
    down_got, up_got = links.data(down_sent, 1), links.half(up_sent)
    draws = lax.optimization_barrier((*draws, down_sent, up_sent, result_far_near))[:2]
    qk_own, qk_other, value_out = last_gradients(a_first, dattn, *draws, own[6], other[6])
    value_out = Reduction(links, value_out)
    value_out_sent = value_out.send(0)
    qk_got, value_out_got = links.half(qk_other), links.data(value_out_sent, 0)
    da1_part = dot(draws[0], qk_cat, 0, 0) + dot(draws[1], value_cat, 0, 0)
    da1_sent = peer_rows(da1_part)
    da1_peer = links.core(da1_sent)
    down.take(hold(down_got, da1_sent))
    up.take(hold(up_got, da1_sent))
    mlp = Reduction(links, jnp.zeros((width, 1), F32))
    mlp.left, mlp.array = list(down.left), jnp.concatenate([down.array, up.array], axis=-1)
    last_bits = list(mlp.left)
    mlp_sent = mlp.send(last_bits[0])
    mlp_got = links.data(mlp_sent, last_bits[0])
    grad_mine, first_sums = input_back(
        jnp.full((1,), core, jnp.int32), hold(da1_part, mlp_sent), da1_peer, x_win, dh, vec_params
    )
    grad_near = links.core(grad_mine)

    value_out.take(hold(value_out_got, grad_mine))
    value_out_sent = value_out.send(1)
    value_out_got = links.data(value_out_sent, 1)
    query_key = Reduction(links, qk_own + hold(qk_got, value_out_sent))
    query_key_sent = query_key.send(0)
    query_key_got = links.data(query_key_sent, 0)
    value_out.take(hold(value_out_got, query_key_sent, mlp_got))
    value_out_sent = value_out.send("half")
    value_out_got = links.half(value_out_sent)
    query_key.take(query_key_got)
    query_key_sent = query_key.send(1)
    query_key_got = links.data(query_key_sent, 1)
    value_out_got = hold(value_out_got, query_key_sent)
    value_out.take(value_out_got)
    grad_far = links.half(hold(grad_mine, value_out_got))
    query_key.take(query_key_got)
    last = Reduction(links, jnp.zeros((width, 1), F32))
    last.left = list(last_bits)
    last.array = jnp.concatenate([query_key.array, value_out.array], axis=-1)
    last_sent = last.send(last_bits[0])
    last_got = links.data(last_sent, last_bits[0])
    mlp.take(mlp_got)
    for bit in last_bits[1:]:
        mlp.step(bit)
    down_share, up_share = mlp.array[:, :units], mlp.array[:, units:]
    one = jnp.ones((1,), F32)
    result = join_sequence(
        links, hold(result_mine, grad_mine), result_near, result_far, result_far_near, parting, seq_len,
        window, one, vec_params[5:6],
    )
    last.take(hold(last_got, result))
    while last.left:
        last.step(last.left[0])
    last_share = last.array

    core_index = jnp.full((1,), core, jnp.int32)
    mine, away = pack_small(
        core_index, first_sums, row_sums, kept, attn_sums, mlp_sq.reshape(1), own_sums, other_sums,
        upb_sums, upb_sums_other,
    )
    summed = mine + links.half(away)
    shared = summed[:8]
    shared = shared + links.core(shared)
    summed = links.sum_data(jnp.concatenate([shared, summed[8:]], axis=0))
    vec_grad = summed[:6]
    stats = summed[6, :3]
    tail = summed[8:].reshape(-1)
    head_grad = tail[: head_params.size].reshape(head_params.shape)
    head_rows = -(-own_sums.shape[1] // width)
    bup_grad = tail[head_rows * width : head_rows * width + units]
    count = stats[0]
    scale = seq_len * links.dp_size / count
    rows = width // links.dp_size
    first_row = links.dp * rows
    shares = (
        jnp.stack([last_share[:, k * group : (k + 1) * group] for k in range(3)]),
        last_share[:, 3 * group :].T,
        up_share,
        down_share,
    )
    old_shares = (
        lax.dynamic_slice_in_dim(qkv_weight, first_row, rows, 1),
        lax.dynamic_slice_in_dim(out_weight, first_row, rows, 1),
        lax.dynamic_slice_in_dim(up_weight, first_row, rows, 0),
        lax.dynamic_slice_in_dim(down_weight, first_row, rows, 1).T,
    )
    first_dp = links.dp == 0
    first_mp = links.mp == 0
    big_sq = jnp.sum(last_share * last_share) + jnp.sum(mlp.array * mlp.array)
    split_sq = jnp.sum(head_grad * head_grad) + jnp.sum(bup_grad * bup_grad)
    whole_sq = jnp.sum(vec_grad * vec_grad)
    raw_sq = (
        big_sq + jnp.where(first_dp, split_sq, 0.0) + jnp.where(first_dp & first_mp, whole_sq, 0.0)
    )
    sq_total = links.sum_all(raw_sq)
    grad_norm = scale * jnp.sqrt(sq_total)
    factor = jnp.minimum(1.0, CLIP_LIMIT / (grad_norm + 1e-06)) * scale
    steps_f = step_count[0].astype(F32)
    corr_one = 1.0 - BETA_ONE**steps_f
    corr_two = 1.0 - BETA_TWO**steps_f
    grad_far = hold(grad_far, sq_total)
    grad_input = join_sequence(
        links, grad_mine, grad_near, grad_far, links.core(grad_far), parting, seq_len, window, scale.reshape(1), jnp.zeros((1, width), F32)
    )
    new_qkv, new_out, new_up, new_down, new_head, new_upb, new_vec = update(
        jnp.stack([factor, corr_one, corr_two]),
        [
            (old_shares[0], shares[0], qkv_first, qkv_second),
            (old_shares[1], shares[1], out_first, out_second),
            (old_shares[2], shares[2], up_first, up_second),
            (old_shares[3], shares[3], down_first.T, down_second.T),
            (head_params, head_grad, head_first, head_second),
            [x.reshape(1, units) for x in (up_bias, bup_grad, upb_first, upb_second)],
            (vec_params, vec_grad, vec_first, vec_second),
        ],
        (WEIGHT_DECAY,) * 4 + (0.0,) * 3,
    )
    new_down = [array.T for array in new_down]
    new_upb = [array.reshape(units) for array in new_upb]
    rms = jnp.sqrt(stats[1:] / (count * width))
    return (
        result, grad_input, *new_qkv, *new_out, *new_up, *new_down, *new_head, *new_upb, *new_vec,
        grad_norm.reshape(1), rms,
    )


def solution(mesh):
    seq = P("dp", None, None)
    row = P("dp", None)
    qkv = P(None, "dp", "mp")
    out = P("mp", "dp")
    up = P("dp", "mp")
    head = P(None, "mp", None)
    unit = P("mp")
    whole = P()
    return jax.shard_map(
        local,
        mesh=mesh,
        in_specs=(
            *(seq, seq, row, row, whole),
            *(P(None, None, "mp"), qkv, qkv),
            *(P("mp", None), out, out),
            *(P(None, "mp"), up, up),
            *(P("mp", None), out, out),
            *(head, head, head),
            *(unit, unit, unit),
            *(whole, whole, whole),
        ),
        out_specs=(
            *(seq, seq),
            *(qkv, qkv, qkv),
            *(out, out, out),
            *(up, up, up),
            *(out, out, out),
            *(head, head, head),
            *(unit, unit, unit),
            *(whole, whole, whole),
            *(whole, whole),
        ),
        check_vma=False,
    )
```

time: 1100 us -> 426 us (0.39)
  waiting for transfers between devices: 586 us -> 73.5 us
  matrix products: 205 us -> 9.54 us
  Pallas kernels: 0 us -> 184 us
  other arithmetic: 164 us -> 42.3 us
  blocking collectives: 80.9 us -> 0 us
  starting transfers between devices: 0.42 us -> 46.8 us
  local copies, waits for them, and re-layouts: 32 us -> 53 us
  between operations: 24.3 us -> 10.9 us
    psum x4 -> x0, waiting for transfers between devices: 586 us -> none  [the longest x1 184 us: local(): lax.psum(jnp.dot(gated, down_low, preferred_element_type=jnp.float32), 'mp')]
    dot_general x35 -> x4, matrix products: 203 us -> 9.54 us  [dot(): lax.dot_general(left, right, (((left_dim,), (right_dim,)), ((), ())), pre...]
    pallas_call x0 -> x17, Pallas kernels: none -> 184 us  [the longest x2 48.7 us: attention_back(): pl.pallas_call(functools.partial(attention_back_kernel, heads, dim), grid...]
    reduce_sum x26 -> x3, other arithmetic: 91.9 us -> 7.61 us  [the longest x1 5.08 us: local(): mlp_sq = jnp.sum(my_rows(kept[:, :1]) * mlp_mine * mlp_mine)]
    psum x2 -> x0, blocking collectives: 80.9 us -> none  [the longest x1 41.8 us: local(): count, attn_total, mlp_total = lax.psum((count_here, attn_sq, mlp_sq), 'dp')]
    ppermute x0 -> x45, waiting for transfers between devices: none -> 73.5 us  [the longest x22 62 us: data(): lax.ppermute(array, 'dp', [(i, i ^ 1 << bit) for i in range(self.dp_size)])]
    ppermute x0 -> x45, starting transfers between devices: none -> 46.8 us  [the longest x22 27.8 us: data(): lax.ppermute(array, 'dp', [(i, i ^ 1 << bit) for i in range(self.dp_size)])]
    convert_element_type x9 -> x0, other arithmetic: 38.7 us -> none  [the longest x4 33.6 us: local(): grad_scores = (probs_full * (grad_probs - delta)).astype(jnp.bfloat16)]
  transfers between devices with their start and end apart: 4 -> 45, of which waited for: 4 -> 16; matrix products, arithmetic and copies ran while one was open for 7% -> 20% of each run, Pallas kernels for 0% -> 37%
where the time goes in v1:
time: 426 us; the launch traced here: 420 us
  Pallas kernels  184 us (43%)
  waiting for transfers between devices  73.5 us (17%)
  local copies, waits for them, and re-layouts  53 us (12%)
  starting transfers between devices  46.8 us (11%)
  other arithmetic  42.3 us (10%)
  between operations  10.9 us (3%)
  matrix products  9.54 us (2%)
    ppermute x22, waiting for transfers between devices, data(): lax.ppermute(array, 'dp', [(i, i ^ 1 << bit) for i in range(self.dp_size)])  62 us
    pallas_call x2, Pallas kernels, attention_back(): pl.pallas_call(functools.partial(attention_back_kernel, heads, dim), grid...  48.7 us
    pallas_call x2, Pallas kernels, attention(): pl.pallas_call(functools.partial(attention_kernel, heads, dim), out_shape...  29.4 us
    ppermute x22, starting transfers between devices, data(): lax.ppermute(array, 'dp', [(i, i ^ 1 << bit) for i in range(self.dp_size)])  27.8 us
    pallas_call x1, Pallas kernels, own_mlp(): pl.pallas_call(own_mlp_kernel, grid=(tokens // BLOCK,), out_shape=[struct...  18.7 us
    ppermute x12, starting transfers between devices, half(): return lax.ppermute(array, 'mp', [(i, i ^ 2) for i in range(self.mp_size)])  16.6 us
    pallas_call x1, Pallas kernels, other_mlp(): pl.pallas_call(other_mlp_kernel, grid=(tokens // BLOCK,), out_shape=[stru...  16.3 us
    add x11, other arithmetic, take(): self.array = self.kept + arrived  14.9 us
  transfers between devices with their start and end apart: 45, of which 16 were waited for; matrix products, arithmetic and copies ran while one was open for 20% of the time, Pallas kernels for 37%

profile of v1, /device:TPU:0, one launch (start us, length us, event | category | flops | bytes accessed | tf_op | source)
XLA Modules:
  0.0 420.0 jit_solution(1101829115715243097)
XLA Ops:
  11.7 8.8 %heads_own.1 = (bf16[1280,768]{1,0:T(8,128)(2,1)}, bf16[192,1280]{1,0:T(8,128)(2,1)}, bf16[192,1280]{1,0:T(8,128)(2,1)}, bf16[192,1280]{1,0:T(8,128)(2,1)}, bf16...) custom-call(bf16[1280,768]{1,0:T(8,128)(2,1)} %dynamic-slice_bitcast_fusion.3.x_ref, ...), custom_call_target="tpu_custom_call" | custom-call | flops 1132462080 | bytes 7864320 | tf_op jit(solution)/shard_map/heads_own/pallas_call | solution.py:353
  29.9 14.7 %attention.2 = (bf16[192,1280]{1,0:T(8,128)(2,1)}, f32[24,1280]{1,0:T(8,128)}) custom-call(s32[8,128]{1,0:T(8,128)} %get-tuple-element.134.plan_ref, bf16[192,1280]{1,0:T(8,128)(2,1)} %get-tuple-element.137.q_ref, bf16[192,1280]{1,0:T(8,128)(2,1)} %get-tuple-element.138.k_ref, bf16[192,1280]{1,0:T(8,128)(2,1)} %get-tuple-element.139.v_ref, ...), custom_call_target="tpu_custom_call" | custom-call | flops 754974720 | bytes 1966080 | tf_op jit(solution)/shard_map/attention/pallas_call | solution.py:387
  45.4 7.6 %heads_other.1 = (bf16[192,1280]{1,0:T(8,128)(2,1)}, bf16[192,1280]{1,0:T(8,128)(2,1)}, bf16[192,1280]{1,0:T(8,128)(2,1)}, bf16[192,1280]{1,0:T(8,128)(2,1)}, bf...) custom-call(s32[4]{0:T(128)} %pad_add_fusion.1.spots_ref, ...), custom_call_target="tpu_custom_call" | custom-call | flops 1132462080 | bytes 7864320 | tf_op jit(solution)/shard_map/heads_other/pallas_call | solution.py:370
  57.3 14.7 %attention.3 = (bf16[192,1280]{1,0:T(8,128)(2,1)}, f32[24,1280]{1,0:T(8,128)}) custom-call(s32[8,128]{1,0:T(8,128)} %get-tuple-element.134.plan_ref, bf16[192,1280]{1,0:T(8,128)(2,1)} %get-tuple-element.151.q_ref, bf16[192,1280]{1,0:T(8,128)(2,1)} %get-tuple-element.152.k_ref, bf16[192,1280]{1,0:T(8,128)(2,1)} %get-tuple-element.153.v_ref, ...), custom_call_target="tpu_custom_call" | custom-call | flops 754974720 | bytes 1966080 | tf_op jit(solution)/shard_map/attention/pallas_call | solution.py:387
  72.8 5.9 %out_project.1.mine_ref = f32[1280,768]{1,0:T(8,128)} custom-call(bf16[192,1280]{1,0:T(8,128)(2,1)} %get-tuple-element.142.o_own_ref.o_ref, bf16[192,1280]{1,0:T(8,128)(2,1)} %get-tuple-element.155.o_other_ref.o_ref, f32[192,768]{1,0:T(8,128)} %out_own_ref.1, f32[192,768]{1,0:T(8,128)} %copy-done.16), custom_call_target="tpu_custom_call" | custom-call | flops 754974720 | bytes 5898240 | tf_op jit(solution)/shard_map/out_project/pallas_call | solution.py:402
  86.4 18.7 %mlp_own.1 = (f32[1280,768]{1,0:T(8,128)}, bf16[1280,768]{1,0:T(8,128)(2,1)}, bf16[1280,768]{1,0:T(8,128)(2,1)}, bf16[1280,1536]{1,0:T(8,128)(2,1)}, bf16[1280,1...) custom-call(bf16[1280,768]{1,0:T(8,128)(2,1)} %dynamic-slice_bitcast_fu, ...), custom_call_target="tpu_custom_call" | custom-call | flops 6039797760 | bytes 39321600 | tf_op jit(solution)/shard_map/mlp_own/pallas_call | solution.py:636
  110.8 16.3 %mlp_other.1 = (bf16[1280,1536]{1,0:T(8,128)(2,1)}, bf16[1280,1536]{1,0:T(8,128)(2,1)}, f32[1280,768]{1,0:T(8,128)}, f32[1280,768]{1,0:T(8,128)}, f32[1,768]{1,0:T(1,128)}) custom-call(s32[4]{0:T(128)} %pad_add_fusion.1.spots_ref, ...), custom_call_target="tpu_custom_call", output_to_operand_aliasing={{2}: (3, {}), {3}: (4, {}), {0}: (11, {}), {1}: (12, {})} | custom-call | flops 6039797760 | bytes 27525120 | tf_op jit(solution)/shard_map/mlp_other/pallas_call | solution.py:675
  147.3 5.1 %fusion = (f32[]{:T(128)}, f32[640,768]{1,0:T(8,128)}) fusion(f32[768]{0:T(1024)S(1)} %get-tuple-element.269, f32[640]{0:T(1024)S(1)} %dynamic-slice_reduce_fusion, f32[640,768]{1,0:T(8,128)} %collective-permute-done.12, f32[1280,768]{1,0:T(8,128)} %get-tuple-element.167, s32[]{:T(128)S(6)} %select_n.96, f32[1280,768]{1,0:T(8,128)} %get-tuple-element.174.hidden_ref), kind=kLoop, calls=%fused_computation.8 | loop fusion | flops 2949119 | bytes 7869960 | tf_op jit(solution)/shard_map/reduce_sum | solution.py:1038
  154.2 12.3 %hidden_back.1 = (f32[1280,768]{1,0:T(8,128)}, bf16[1280,768]{1,0:T(8,128)(2,1)}, bf16[192,1280]{1,0:T(8,128)(2,1)}, bf16[192,1280]{1,0:T(8,128)(2,1)}, f32[4,768]{1,0:T(4,128)}) custom-call(f32[1280,768]{1,0:T(8,128)} %get-tuple-element.174.hidden_ref, f32[1280,768]{1,0:T(8,128)} %get-tuple-element.175.mine_ref, ...), custom_call_target="tpu_custom_call" | custom-call | flops 754974720 | bytes 21626880 | tf_op jit(solution)/shard_map/hidden_back/pallas_call | solution.py:740
  166.5 19.2 %attention_back.2 = (bf16[768,1280]{1,0:T(8,128)(2,1)}, bf16[384,1280]{1,0:T(8,128)(2,1)}, f32[1,1024]{1,0:T(1,128)}) custom-call(s32[8,128]{1,0:T(8,128)} %get-tuple-element.134.plan_ref, bf16[192,1280]{1,0:T(8,128)(2,1)} %get-tuple-element.137.q_ref, bf16[192,1280]{1,0:T(8,128)(2,1)} %get-tuple-element.138.k_ref, ...), custom_call_target="tpu_custom_call" | custom-call | flops 1887436800 | bytes 7372800 | tf_op jit(solution)/shard_map/attention_back/pallas_call | solution.py:501
  185.7 5.3 %collective-permute-done.15 = f32[2,2,96,1536]{3,2,1,0:T(8,128)S(1)} collective-permute-done((f32[2,2,96,1536]{3,2,1,0:T(8,128)}, f32[2,2,96,1536]{3,2,1,0:T(8,128)S(1)}, u32[]{:S(2)}, u32[]{:S(2)}) %collective-permute-start.15) | collective-permute-done | bytes 2359328 | tf_op jit(solution)/shard_map/ppermute | solution.py:53
  192.5 6.3 %collective-permute-done.14 = f32[2,2,96,1536]{3,2,1,0:T(8,128)} collective-permute-done((f32[2,2,96,1536]{3,2,1,0:T(8,128)}, f32[2,2,96,1536]{3,2,1,0:T(8,128)}, u32[]{:S(2)}, u32[]{:S(2)}) %collective-permute-start.14) | collective-permute-done | bytes 2359328 | tf_op jit(solution)/shard_map/ppermute | solution.py:53
  209.9 29.4 %attention_back.3 = (bf16[768,1280]{1,0:T(8,128)(2,1)}, bf16[384,1280]{1,0:T(8,128)(2,1)}, f32[1,1024]{1,0:T(1,128)}) custom-call(s32[8,128]{1,0:T(8,128)} %get-tuple-element.134.plan_ref, bf16[192,1280]{1,0:T(8,128)(2,1)} %get-tuple-element.151.q_ref, bf16[192,1280]{1,0:T(8,128)(2,1)} %get-tuple-element.152.k_ref, ...), custom_call_target="tpu_custom_call", output_to_operand_aliasing={{0}: (13, {}), {1}: (14, {})} | custom-call | flops 1887436800 | bytes 7372800 | tf_op jit(solution)/shard_map/attention_back/pallas_call | solution.py:501
  252.4 7.8 %last_gradients.1 = (f32[768,384]{1,0:T(8,128)}, f32[768,384]{1,0:T(8,128)}, f32[768,768]{1,0:T(8,128)}) custom-call(bf16[1280,768]{1,0:T(8,128)(2,1)} %get-tuple-element.143.a_ref, bf16[1280,768]{1,0:T(8,128)(2,1)} %get-tuple-element.211.dattn_ref, bf16[768,1280]{1,0:T(8,128)(2,1)} %get-tuple-element.192.qk_ref, ...), custom_call_target="tpu_custom_call" | custom-call | flops 3019898880 | bytes 11796480 | tf_op jit(solution)/shard_map/last_gradients/pallas_call | solution.py:865
  263.0 3.5 collective-permute-done.22
  272.3 6.6 %collective-permute-start.33 = (f32[96,1536]{1,0:T(8,128)}, f32[96,1536]{1,0:T(8,128)}, u32[]{:S(2)}, u32[]{:S(2)}) collective-permute-start(f32[96,1536]{1,0:T(8,128)} %fusion.6), channel_id=1, source_target_pairs={{0,16},{4,20},{8,24},{12,28},{16,0},{20,4},{24,8},{28,12},{1,17},{... | collective-permute-start | bytes 1769480 | tf_op jit(solution)/shard_map/ppermute | solution.py:53
  278.9 6.3 %input_back.1 = (f32[640,768]{1,0:T(8,128)}, f32[2,768]{1,0:T(2,128)}) custom-call(s32[1]{0:T(128)} %bitcast.core_ref, f32[1280,768]{1,0:T(8,128)} %copy-done.4, f32[640,768]{1,0:T(8,128)} %collective-permute-done.23.peer_ref, bf16[1280,768]{1,0:T(8,128)(2,1)} %dynamic-slice_bitcast_fusion.3.x_ref, f32[1280,768]{1,0:T(8,128)} %get-tuple-element.199.dh_ref, ...), custom_call_target="tpu_custom_call" | custom-call | bytes 8847360 | tf_op jit(solution)/shard_map/input_back/pallas_call | solution.py:788
  285.2 5.3 %collective-permute-done.30 = f32[2,2,96,768]{3,2,1,0:T(8,128)} collective-permute-done((f32[2,2,96,768]{3,2,1,0:T(8,128)}, f32[2,2,96,768]{3,2,1,0:T(8,128)}, u32[]{:S(2)}, u32[]{:S(2)}) %collective-permute-start.30) | collective-permute-done | bytes 1179680 | tf_op jit(solution)/shard_map/ppermute | solution.py:53
  304.4 12.5 %collective-permute-done.31 = f32[2,96,768]{2,1,0:T(8,128)} collective-permute-done((f32[2,96,768]{2,1,0:T(8,128)S(1)}, f32[2,96,768]{2,1,0:T(8,128)}, u32[]{:S(2)}, u32[]{:S(2)}) %collective-permute-start.31) | collective-permute-done | bytes 589856 | tf_op jit(solution)/shard_map/ppermute | solution.py:53
  320.4 6.7 %collective-permute-done.34 = f32[2,96,384]{2,1,0:T(8,128)S(1)} collective-permute-done((f32[2,96,384]{2,1,0:T(8,128)S(1)}, f32[2,96,384]{2,1,0:T(8,128)S(1)}, u32[]{:S(2)}, u32[]{:S(2)}) %collective-permute-start.34) | collective-permute-done | bytes 294944 | tf_op jit(solution)/shard_map/ppermute | solution.py:50
  337.0 6.5 %join_sequence.2 = bf16[1,2048,768]{2,1,0:T(8,128)(2,1)} custom-call(s32[3]{0:T(128)} %pad_add_fusion.info_ref, f32[1]{0:T(128)} %constant.130.clone.1.factor_ref, f32[1,768]{1,0:T(1,128)} %get-tuple-element.270.shift_ref, f32[640,768]{1,0:T(8,128)} %get-tuple-element.201.mine_ref, f32[640,768]{1,0:T(8,128)} %collective-permute-done.17.near_ref, ...), custom_call_target="tpu_custom_call" | custom-call | bytes 11010048 | tf_op jit(solution)/shard_map/join_sequence/pallas_call | solution.py:835
  350.7 15.7 %collective-permute-done.38 = f32[96,768]{0,1:T(8,128)S(1)} collective-permute-done((f32[96,768]{0,1:T(8,128)S(1)}, f32[96,768]{0,1:T(8,128)S(1)}, u32[]{:S(2)}, u32[]{:S(2)}) %collective-permute-start.38) | collective-permute-done | bytes 294944 | tf_op jit(solution)/shard_map/ppermute | solution.py:53
  403.6 4.1 update.1
  412.1 6.5 %join_sequence.3 = bf16[1,2048,768]{2,1,0:T(8,128)(2,1)} custom-call(s32[3]{0:T(128)} %pad_add_fusion.info_ref, f32[1]{0:T(128)} %bitcast.32.factor_ref, f32[1,768]{1,0:T(1,128)} %broadcast_in_dim.2.shift_ref, f32[640,768]{1,0:T(8,128)} %get-tuple-element.219.mine_ref, f32[640,768]{1,0:T(8,128)} %collective-permute-done.29.near_ref, ...), custom_call_target="tpu_custom_call" | custom-call | bytes 11010048 | tf_op jit(solution)/shard_map/join_sequence/pallas_call | solution.py:835
  (247 shorter events, 163.1 us)
Async XLA Ops:
  20.5 32.4 %collective-permute-start.5 = (f32[2,192,768]{2,1,0:T(8,128)S(1)}, f32[2,192,768]{2,1,0:T(8,128)S(1)}, u32[]{:S(2)}, u32[]{:S(2)}) collective-permute-start(f32[2,192,768]{2,1,0:T(8,128)S(1)} %copy-done.27), channel_id=1, source_target_pairs={{0,2},{1,3},{2,0},{3,1},{4,6},{5,7},{6,4},{7,5},{8,10},{9,11},{10,... | collective-permute-start | bytes 3538952 | tf_op jit(solution)/shard_map/ppermute | solution.py:50
  22.6 22.0 %collective-permute-start.1 = (f32[3,48,768]{2,1,0:T(8,128)}, f32[3,48,768]{2,1,0:T(8,128)S(1)}, u32[]{:S(2)}, u32[]{:S(2)}) collective-permute-start(f32[3,48,768]{2,1,0:T(8,128)} %collective-permute-done.p0), channel_id=1, source_target_pairs={{0,4},{4,0},{8,12},{12,8},{16,20},{20,16},{24,28},{28,24},{1,5},{5... | collective-permute-start | bytes 1327112 | tf_op jit(solution)/shard_map/ppermute | solution.py:53
  24.1 20.5 %collective-permute-start.2 = (f32[3,48,768]{2,1,0:T(8,128)}, f32[3,48,768]{2,1,0:T(8,128)}, u32[]{:S(2)}, u32[]{:S(2)}) collective-permute-start(f32[3,48,768]{2,1,0:T(8,128)} %collective-permute-done.p0), channel_id=1, source_target_pairs={{0,8},{4,12},{8,0},{12,4},{16,24},{20,28},{24,16},{28,20},{1,9},{5... | collective-permute-start | bytes 1327112 | tf_op jit(solution)/shard_map/ppermute | solution.py:53
  25.6 19.0 %collective-permute-start.3 = (f32[3,48,768]{2,1,0:T(8,128)}, f32[3,48,768]{2,1,0:T(8,128)}, u32[]{:S(2)}, u32[]{:S(2)}) collective-permute-start(f32[3,48,768]{2,1,0:T(8,128)} %collective-permute-done.p0), channel_id=1, source_target_pairs={{0,12},{4,8},{8,4},{12,0},{16,28},{20,24},{24,20},{28,16},{1,13},{... | collective-permute-start | bytes 1327112 | tf_op jit(solution)/shard_map/ppermute | solution.py:990
  79.9 28.6 %collective-permute-start.10 = (f32[2,2,96,768]{3,2,1,0:T(8,128)}, f32[2,2,96,768]{3,2,1,0:T(8,128)S(1)}, u32[]{:S(2)}, u32[]{:S(2)}) collective-permute-start(f32[2,2,96,768]{3,2,1,0:T(8,128)} %pad_maximum_fusion), channel_id=1, source_target_pairs={{0,8},{4,12},{8,0},{12,4},{16,24},{20,28},{24,16},{28,20},{1,9},{5... | collective-permute-start | bytes 3538952 | tf_op jit(solution)/shard_map/ppermute | solution.py:53
  82.1 28.7 %collective-permute-start.11 = (f32[2,2,96,768]{3,2,1,0:T(8,128)}, f32[2,2,96,768]{3,2,1,0:T(8,128)}, u32[]{:S(2)}, u32[]{:S(2)}) collective-permute-start(f32[2,2,96,768]{3,2,1,0:T(8,128)} %pad_maximum_fusion.1), channel_id=1, source_target_pairs={{0,4},{4,0},{8,12},{12,8},{16,20},{20,16},{24,28},{28,24},{1,5},{5... | collective-permute-start | bytes 3538952 | tf_op jit(solution)/shard_map/ppermute | solution.py:53
  127.1 27.1 %collective-permute-start.13 = (f32[1280,768]{1,0:T(8,128)}, f32[1280,768]{1,0:T(8,128)}, u32[]{:S(2)}, u32[]{:S(2)}) collective-permute-start(f32[1280,768]{1,0:T(8,128)} %get-tuple-element.175.mine_ref), channel_id=1, source_target_pairs={{0,1},{1,0},{2,3},{3,2},{4,5},{5,4},{6,7},{7,6},{8,9},{9,8},{10,11... | collective-permute-start | bytes 11796488 | tf_op jit(solution)/shard_map/ppermute | solution.py:47
  137.7 53.4 %collective-permute-start.15 = (f32[2,2,96,1536]{3,2,1,0:T(8,128)}, f32[2,2,96,1536]{3,2,1,0:T(8,128)S(1)}, u32[]{:S(2)}, u32[]{:S(2)}) collective-permute-start(f32[2,2,96,1536]{3,2,1,0:T(8,128)} %dynamic-slice_bitcast_fusion), channel_id=1, source_target_pairs={{0,8},{4,12},{8,0},{12,4},{16,24},{20,28},{24,16},{28,20},{1,9},{5... | collective-permute-start | bytes 7077896 | tf_op jit(solution)/shard_map/ppermute | solution.py:53
  145.5 53.2 %collective-permute-start.14 = (f32[2,2,96,1536]{3,2,1,0:T(8,128)}, f32[2,2,96,1536]{3,2,1,0:T(8,128)}, u32[]{:S(2)}, u32[]{:S(2)}) collective-permute-start(f32[2,2,96,1536]{3,2,1,0:T(8,128)} %dynamic-slice_bitcast_fusion.1), channel_id=1, source_target_pairs={{0,4},{4,0},{8,12},{12,8},{16,20},{20,16},{24,28},{28,24},{1,5},{5... | collective-permute-start | bytes 7077896 | tf_op jit(solution)/shard_map/ppermute | solution.py:53
  152.4 50.5 %collective-permute-start.16 = (f32[640,768]{1,0:T(8,128)}, f32[640,768]{1,0:T(8,128)}, u32[]{:S(2)}, u32[]{:S(2)}) collective-permute-start(f32[640,768]{1,0:T(8,128)} %get-tuple-element.201.mine_ref), channel_id=1, source_target_pairs={{0,2},{1,3},{2,0},{3,1},{4,6},{5,7},{6,4},{7,5},{8,10},{9,11},{10,... | collective-permute-start | bytes 5898248 | tf_op jit(solution)/shard_map/ppermute | solution.py:50
  154.2 55.7 %collective-permute-start.17 = (f32[640,768]{1,0:T(8,128)}, f32[640,768]{1,0:T(8,128)}, u32[]{:S(2)}, u32[]{:S(2)}) collective-permute-start(f32[640,768]{1,0:T(8,128)} %get-tuple-element.201.mine_ref), channel_id=1, source_target_pairs={{0,1},{1,0},{2,3},{3,2},{4,5},{5,4},{6,7},{7,6},{8,9},{9,8},{10,11... | collective-permute-start | bytes 5898248 | tf_op jit(solution)/shard_map/ppermute | solution.py:47
  202.6 36.7 %collective-permute-start.19 = (f32[2,96,1536]{2,1,0:T(8,128)}, f32[2,96,1536]{2,1,0:T(8,128)}, u32[]{:S(2)}, u32[]{:S(2)}) collective-permute-start(f32[2,96,1536]{2,1,0:T(8,128)} %dynamic-slice_bitcast_fusion.5), channel_id=1, source_target_pairs={{0,4},{4,0},{8,12},{12,8},{16,20},{20,16},{24,28},{28,24},{1,5},{5... | collective-permute-start | bytes 3538952 | tf_op jit(solution)/shard_map/ppermute | solution.py:53
  202.9 41.5 %collective-permute-start.20 = (f32[640,768]{1,0:T(8,128)}, f32[640,768]{1,0:T(8,128)}, u32[]{:S(2)}, u32[]{:S(2)}) collective-permute-start(f32[640,768]{1,0:T(8,128)} %collective-permute-done.16.far_ref), channel_id=1, source_target_pairs={{0,1},{1,0},{2,3},{3,2},{4,5},{5,4},{6,7},{7,6},{8,9},{9,8},{10,11... | collective-permute-start | bytes 5898248 | tf_op jit(solution)/shard_map/ppermute | solution.py:47
  208.2 33.7 %collective-permute-start.18 = (f32[2,2,96,768]{3,2,1,0:T(8,128)}, f32[2,2,96,768]{3,2,1,0:T(8,128)}, u32[]{:S(2)}, u32[]{:S(2)}) collective-permute-start(f32[2,2,96,768]{3,2,1,0:T(8,128)} %slice.130), channel_id=1, source_target_pairs={{0,2},{1,3},{2,0},{3,1},{4,6},{5,7},{6,4},{7,5},{8,10},{9,11},{10,... | collective-permute-start | bytes 3538952 | tf_op jit(solution)/shard_map/ppermute | solution.py:50
  250.6 28.4 %collective-permute-start.23 = (f32[640,768]{1,0:T(8,128)}, f32[640,768]{1,0:T(8,128)}, u32[]{:S(2)}, u32[]{:S(2)}) collective-permute-start(f32[640,768]{1,0:T(8,128)} %constant_dynamic-slice_fusion.4), channel_id=1, source_target_pairs={{0,1},{1,0},{2,3},{3,2},{4,5},{5,4},{6,7},{7,6},{8,9},{9,8},{10,11... | collective-permute-start | bytes 5898248 | tf_op jit(solution)/shard_map/ppermute | solution.py:47
  262.6 27.9 %collective-permute-start.30 = (f32[2,2,96,768]{3,2,1,0:T(8,128)}, f32[2,2,96,768]{3,2,1,0:T(8,128)}, u32[]{:S(2)}, u32[]{:S(2)}) collective-permute-start(f32[2,2,96,768]{3,2,1,0:T(8,128)} %dynamic-slice_bitcast_fusion.4), channel_id=1, source_target_pairs={{0,4},{4,0},{8,12},{12,8},{16,20},{20,16},{24,28},{28,24},{1,5},{5... | collective-permute-start | bytes 3538952 | tf_op jit(solution)/shard_map/ppermute | solution.py:53
  267.4 31.5 %collective-permute-start.32 = (f32[768,384]{1,0:T(8,128)}, f32[768,384]{1,0:T(8,128)}, u32[]{:S(2)}, u32[]{:S(2)}) collective-permute-start(f32[768,384]{1,0:T(8,128)} %get-tuple-element.215), channel_id=1, source_target_pairs={{0,2},{1,3},{2,0},{3,1},{4,6},{5,7},{6,4},{7,5},{8,10},{9,11},{10,... | collective-permute-start | bytes 3538952 | tf_op jit(solution)/shard_map/ppermute | solution.py:50
  272.3 32.1 %collective-permute-start.33 = (f32[96,1536]{1,0:T(8,128)}, f32[96,1536]{1,0:T(8,128)}, u32[]{:S(2)}, u32[]{:S(2)}) collective-permute-start(f32[96,1536]{1,0:T(8,128)} %fusion.6), channel_id=1, source_target_pairs={{0,16},{4,20},{8,24},{12,28},{16,0},{20,4},{24,8},{28,12},{1,17},{... | collective-permute-start | bytes 1769480 | tf_op jit(solution)/shard_map/ppermute | solution.py:53
  292.3 24.6 %collective-permute-start.31 = (f32[2,96,768]{2,1,0:T(8,128)S(1)}, f32[2,96,768]{2,1,0:T(8,128)}, u32[]{:S(2)}, u32[]{:S(2)}) collective-permute-start(f32[2,96,768]{2,1,0:T(8,128)S(1)} %dynamic-slice_bitcast_fusion.7), channel_id=1, source_target_pairs={{0,8},{4,12},{8,0},{12,4},{16,24},{20,28},{24,16},{28,20},{1,9},{5... | collective-permute-start | bytes 1769480 | tf_op jit(solution)/shard_map/ppermute | solution.py:53
  302.1 25.6 %collective-permute-start.26 = (f32[16,768]{1,0:T(8,128)S(1)}, f32[16,768]{1,0:T(8,128)S(1)}, u32[]{:S(2)}, u32[]{:S(2)}) collective-permute-start(f32[16,768]{1,0:T(8,128)S(1)} %pad_maximum_fusion.3), channel_id=1, source_target_pairs={{0,4},{4,0},{8,12},{12,8},{16,20},{20,16},{24,28},{28,24},{1,5},{5... | collective-permute-start | bytes 147464 | tf_op jit(solution)/shard_map/ppermute | solution.py:53
  327.1 61.2 %collective-permute-start.36 = (f32[640,768]{1,0:T(8,128)}, f32[640,768]{1,0:T(8,128)}, u32[]{:S(2)}, u32[]{:S(2)}) collective-permute-start(f32[640,768]{1,0:T(8,128)} %get-tuple-element.219.mine_ref), channel_id=1, source_target_pairs={{0,2},{1,3},{2,0},{3,1},{4,6},{5,7},{6,4},{7,5},{8,10},{9,11},{10,... | collective-permute-start | bytes 5898248 | tf_op jit(solution)/shard_map/ppermute | solution.py:50
  337.0 74.5 %collective-permute-start.29 = (f32[640,768]{1,0:T(8,128)}, f32[640,768]{1,0:T(8,128)}, u32[]{:S(2)}, u32[]{:S(2)}) collective-permute-start(f32[640,768]{1,0:T(8,128)} %get-tuple-element.219.mine_ref), channel_id=1, source_target_pairs={{0,1},{1,0},{2,3},{3,2},{4,5},{5,4},{6,7},{7,6},{8,9},{9,8},{10,11... | collective-permute-start | bytes 5898248 | tf_op jit(solution)/shard_map/ppermute | solution.py:47
  346.0 20.4 %collective-permute-start.38 = (f32[96,768]{0,1:T(8,128)S(1)}, f32[96,768]{0,1:T(8,128)S(1)}, u32[]{:S(2)}, u32[]{:S(2)}) collective-permute-start(f32[96,768]{0,1:T(8,128)S(1)} %bitcast.137), channel_id=1, source_target_pairs={{0,16},{4,20},{8,24},{12,28},{16,0},{20,4},{24,8},{28,12},{1,17},{... | collective-permute-start | bytes 884744 | tf_op jit(solution)/shard_map/ppermute | solution.py:53
  388.3 23.2 %collective-permute-start.44 = (f32[640,768]{1,0:T(8,128)}, f32[640,768]{1,0:T(8,128)}, u32[]{:S(2)}, u32[]{:S(2)}) collective-permute-start(f32[640,768]{1,0:T(8,128)} %collective-permute-done.36.far_ref), channel_id=1, source_target_pairs={{0,1},{1,0},{2,3},{3,2},{4,5},{5,4},{6,7},{7,6},{8,9},{9,8},{10,11... | collective-permute-start | bytes 5898248 | tf_op jit(solution)/shard_map/ppermute | solution.py:47
  (58 other events, 484.2 us)
